TPU v7x, 128 devices: a whole 4x4x4 slice. The times are simulated.
128 devices in a mesh: expert: 16 (over z_hi, x, core), dp: 8 (over z_lo, y).
Axes of the slice: x: 4, y: 4, z: 4 (z_hi: 2, z_lo: 2; z = z_hi * 2 + z_lo), core: 2. Of those that a mesh axis runs over, the one named last changes fastest.
Arguments:
- trunk: bfloat16 [3072, 4096], P(('dp', 'expert')), may hold values from -6 to 6
- w_first: bfloat16 [16, 4096, 2048], P('expert'), may hold values from -0.09375 to 0.09375
- w_second: bfloat16 [16, 2048, 1024], P('expert'), may hold values from -0.125 to 0.125
- gates: bfloat16 [16, 8, 3072], P('expert', None, 'dp'), may hold values from 0.049804688 to 1
- d_mixed: bfloat16 [3072, 8, 1024], P(('dp', 'expert')), may hold values from -6 to 6
Outputs:
- mixed: bfloat16 [3072, 8, 1024], P(('dp', 'expert'))
- d_trunk: bfloat16 [3072, 4096], P(('dp', 'expert'))
- d_gates: bfloat16 [16, 8, 3072], P('expert', None, 'dp')
- d_w_first: bfloat16 [16, 4096, 2048], P('expert', 'dp')
- d_w_second: bfloat16 [16, 2048, 1024], P('expert', 'dp')
All inputs are finite; a program needn't handle non-finite values.
Results may differ from a plain program's by a relative error of at most 0.015.
Values may be sent and summed in bfloat16 or wider, within the bound.
No kernel may reach another device: no remote copies, remote signals or barrier semaphores. Data moves between devices by JAX's collectives and lax.ppermute only.
A program may use at most 128 MiB of HBM per device.

v0:
```python
import jax
import jax.numpy as jnp
from jax import lax
from jax.experimental import pallas as pl
from jax.experimental.pallas import tpu as pltpu
from jax.sharding import PartitionSpec as P

AXES = ("expert", "dp")
BF = jnp.bfloat16
F32 = jnp.float32


def coords(i):
    e, d = divmod(i, 8)
    zl, y = divmod(d, 4)
    zh, r = divmod(e, 8)
    x, c = divmod(r, 2)
    return x, y, zh, zl, c


def index(x, y, zh, zl, c):
    return (zh * 8 + x * 2 + c) * 8 + zl * 4 + y


def swap(v, y=0, z=0, c=0):
    pairs = []
    for i in range(128):
        px, py, pzh, pzl, pc = coords(i)
        pairs.append((i, index(px, py ^ y, pzh ^ (z >> 1), pzl ^ (z & 1), pc ^ c)))
    return lax.ppermute(v, AXES, pairs)


def swap_split(v, k, first):
    pairs = []
    for i in range(128):
        px, py, pzh, pzl, pc = coords(i)
        if (pc == 0) == first:
            pzh, pzl = pzh ^ (k & 1), pzl ^ (k >> 1)
        else:
            px = px ^ k
        pairs.append((i, index(px, py, pzh, pzl, pc)))
    return lax.ppermute(v, AXES, pairs)


def after(v, *others):
    return lax.optimization_barrier((v,) + others)[0]


def grid():
    return [[coords(i), i] for i in range(128)]


def groups(key, order):
    rows = {}
    for at, i in grid():
        rows.setdefault(key(*at), []).append((order(*at), i))
    return [[i for _, i in sorted(rows[k])] for k in sorted(rows)]


PLANE = groups(lambda x, y, zh, zl, c: (y, c), lambda x, y, zh, zl, c: (x, zl, zh))
RING = groups(lambda x, y, zh, zl, c: (x, zh, zl, c), lambda x, y, zh, zl, c: y)


def exchange(v, members):
    return lax.all_to_all(v, AXES, 0, 0, axis_index_groups=members, tiled=True)


def dot(a, b, dims):
    return lax.dot_general(a, b, (dims, ((), ())), preferred_element_type=F32)


def pick(a, i, axis):
    return lax.dynamic_index_in_dim(a, i, axis, keepdims=False)


def gather(v, members):
    return exchange(jnp.broadcast_to(v[None], (len(members[0]),) + v.shape), members)


def place_kernel(at, *refs):
    out = refs[4]
    for i in range(16):
        out[at[i]] = refs[i // 4][i % 4]


def place(kernel, shape, at, lines):
    return pl.pallas_call(
        kernel,
        out_shape=jax.ShapeDtypeStruct(shape, lines[0].dtype),
        in_specs=[pl.BlockSpec(memory_space=pltpu.SMEM)]
        + [pl.BlockSpec(memory_space=pltpu.VMEM)] * 4,
        out_specs=pl.BlockSpec(memory_space=pltpu.VMEM),
        compiler_params=pltpu.CompilerParams(vmem_limit_bytes=16 << 20),
        cost_estimate=pl.CostEstimate(flops=0, bytes_accessed=6 << 20, transcendentals=0),
    )(at, *lines)


def on_device(trunk, w_first, w_second, gates, d_mixed):
    e = lax.axis_index("expert")
    d = lax.axis_index("dp")
    zl, y = d // 4, d % 4
    zh, x, c = e // 8, (e % 8) // 2, e % 2
    zz = zl * 2 + zh

    gate_rows = lax.all_to_all(
        gates[0].reshape(8, 16, 24).transpose(1, 0, 2), "expert", 0, 0, tiled=True
    )

    line = jnp.stack([trunk] + [swap_split(trunk, k, True) for k in (1, 2, 3)])
    far = [swap_split(line, k, False) for k in (2, 1, 3)]
    dx, dz = x ^ (jnp.arange(16) // 4), zz ^ (jnp.arange(16) % 4)
    ex, ez = x ^ (jnp.arange(16) % 4), zz ^ (jnp.arange(16) // 4)
    at = jnp.where(c == 0, dx * 4 + dz, ex * 4 + ez).astype(jnp.int32)
    own = place(place_kernel, (16, 24, 4096), at, [line, far[1], far[0], far[2]])
    own = own.reshape(384, 4096)

    d_out_each = jnp.einsum(
        "etr,rto->ero", after(gate_rows, line), d_mixed, preferred_element_type=F32
    ).astype(BF)
    back = lax.all_to_all(d_out_each, "expert", 0, 0, tiled=True)

    trunk, _ = lax.optimization_barrier((trunk, d_out_each))
    half = lax.dynamic_slice_in_dim(w_first[0], zl * 1024, 1024, 1)
    cols = trunk.reshape(24, 2, 4, 512)
    t_y = [pick(cols, y ^ k, 2).reshape(24, 1024) for k in range(4)]
    t_y = jnp.stack([t_y[0]] + [swap(t_y[k], y=k) for k in (1, 3, 2)])

    own, back, t_y = lax.optimization_barrier((own, back, t_y))
    other = swap(own, c=1)
    back = back.reshape(2, 4, 2, 24, 1024)
    back_z = swap(back, z=1)

    second = w_second[0]
    second_own = lax.dynamic_slice_in_dim(second, zl * 1024, 1024, 0)
    second_far = lax.dynamic_slice_in_dim(second, (1 - zl) * 1024, 1024, 0)

    def forward(rows):
        pre = dot(rows, half, ((1,), (0,)))
        sig = jax.nn.sigmoid(pre)
        slope = sig * (1.0 + pre * (1.0 - sig))
        return (pre * sig).astype(BF), slope

    def backward(d_o, slope):
        d_hidden = dot(d_o, second_own, ((1,), (1,)))
        return (d_hidden * slope).astype(BF)

    hidden_own, slope_own = forward(own)
    hidden_own, back_z, t_y = lax.optimization_barrier((hidden_own, back_z, t_y))
    wide = gather(t_y, PLANE)
    pair = jnp.where(zl == 0, jnp.stack([back, back_z]), jnp.stack([back_z, back]))
    pair = pair.transpose(3, 2, 0, 1, 4, 5)
    d_output = jnp.where(c == 0, pair, pair[::-1]).reshape(768, 1024)

    d_own = backward(d_output[:384], slope_own)
    d_own, other = lax.optimization_barrier((d_own, other))
    near_own = (swap(d_own, y=1), swap(d_own, y=3))
    hidden_other, slope_other = forward(other)
    d_other = backward(d_output[384:], slope_other)
    near_other = (swap(d_other, y=1), swap(d_other, y=3))
    hidden = jnp.concatenate([hidden_own, hidden_other])
    by_z = hidden.reshape(8, 2, 48, 1024)
    mine = pick(by_z, zl, 1).reshape(384, 1024)
    theirs = swap(pick(by_z, 1 - zl, 1).reshape(384, 1024), z=1)

    d_late, near_own = lax.optimization_barrier((d_other, near_own))
    far_own = swap(near_own[1], y=1)
    dt_other = dot(d_late, half, ((1,), (1,))).astype(BF)
    dt = dot(d_own, half, ((1,), (1,))) + swap(dt_other, c=1).astype(F32)
    dt = dt.astype(BF)

    dt, mine, near_other, wide = lax.optimization_barrier((dt, mine, near_other, wide))
    far_other = swap(near_other[0], y=3)
    output = dot(mine, second_own, ((1,), (0,))) + dot(theirs, second_far, ((1,), (0,)))
    output = output.astype(BF).reshape(2, 4, 2, 24, 1024)
    output = jnp.where(c == 0, output, output[::-1])
    output = output.transpose(2, 1, 0, 3, 4).reshape(16, 24, 1024)
    outs = lax.all_to_all(output, "expert", 0, 0, tiled=True)
    dt, outs, far_own = lax.optimization_barrier((dt, outs, far_own))
    dt = exchange(dt.reshape(16, 24, 4096), PLANE)
    d_trunk = jnp.sum(dt, axis=0, dtype=F32).astype(BF)
    wide = wide.reshape(16, 4, 24, 1024).transpose(1, 0, 2, 3).reshape(1536, 1024)
    wide_other = swap(wide, c=1)

    ds = dot(hidden, d_output, ((0,), (0,))).astype(BF)
    d_second = lax.psum_scatter(
        ds, AXES, axis_index_groups=RING, scatter_dimension=0, tiled=True
    )

    mixed = jnp.einsum(
        "etr,ero->rto", gate_rows, outs, preferred_element_type=F32
    ).astype(BF)
    d_gate = jnp.einsum(
        "rto,ero->etr", d_mixed, outs, preferred_element_type=F32
    ).astype(BF)

    d_gate = lax.all_to_all(after(d_gate, dt), "expert", 0, 0, tiled=True)
    d_gate = d_gate.transpose(1, 0, 2).reshape(8, 384)

    tile = dot(wide[:1152], jnp.concatenate([d_own, *near_own]), ((0,), (0,)))
    tile = tile + dot(wide_other[:1152], jnp.concatenate([d_other, *near_other]), ((0,), (0,)))
    tile = tile + dot(wide[1152:], far_own, ((0,), (0,)))
    tile = tile + dot(wide_other[1152:], far_other, ((0,), (0,)))
    tile = tile.astype(BF).reshape(2, 512, 1024)
    far = swap(pick(tile, 1 - zl, 0), z=1)
    near = pick(tile, zl, 0)
    d_first = jnp.where(
        zl == 0,
        jnp.concatenate([near, far], axis=1),
        jnp.concatenate([far, near], axis=1),
    )
    return (mixed, d_trunk, d_gate[None], d_first[None], d_second[None])


def solution(mesh):
    in_specs = (
        P(("dp", "expert"), None),
        P("expert", None, None),
        P("expert", None, None),
        P("expert", None, "dp"),
        P(("dp", "expert"), None, None),
    )
    out_specs = (
        P(("dp", "expert"), None, None),
        P(("dp", "expert"), None),
        P("expert", None, "dp"),
        P("expert", "dp", None),
        P("expert", "dp", None),
    )
    return jax.shard_map(
        on_device, mesh=mesh, in_specs=in_specs, out_specs=out_specs, check_vma=False
    )
```

profile of v0, /device:TPU:49, one launch (start us, length us, event | category | flops | bytes accessed | tf_op | source)
XLA Modules:
  0.0 303.8 jit_solution(7200623282237878781)
XLA Ops:
  12.3 8.5 %all-to-all-start = ((bf16[16,8,24]{2,1,0:T(8,128)(2,1)}), bf16[16,8,24]{2,1,0:T(8,128)(2,1)}, u32[]{:S(2)}, u32[]{:S(2)}) async-start(bf16[16,8,24]{2,1,0:T(8,128)(2,1)} %copy.35), calls=%async_computation | async-start | bytes 65536 | tf_op jit(solution)/shard_map/all_to_all | solution.py:105
  32.2 5.1 %all-to-all-start.1 = ((bf16[16,24,1024]{2,1,0:T(8,128)(2,1)}), bf16[16,24,1024]{2,1,0:T(8,128)(2,1)}, u32[]{:S(2)}, u32[]{:S(2)}) async-start(bf16[16,24,1024]{2,1,0:T(8,128)(2,1)} %copy.37), calls=%async_computation.1 | async-start | bytes 1572864 | tf_op jit(solution)/shard_map/all_to_all | solution.py:120
  39.0 3.2 %dynamic-slice_reduce_fusion.3 = (bf16[24,2,512]{2,1,0:T(2,128)(2,1)}, bf16[24,2,512]{2,1,0:T(2,128)(2,1)}, bf16[24,2,512]{2,1,0:T(2,128)(2,1)}, bf16[24,2,512]{2,1,0:T(2,128)(2,1)S(1)}) fusion(bf16[24,2,4,512]{3,2,1,0:T(4,128)(2,1)} %reshape.121, s32[]{:T(128)S(6)} %select_n.132, s32[]{:T(128)S(6)} %select_n.134, s32[]{:T(128)S(6)} %select_n.133, ...), kind=kLoop, calls=%fused_computation.71 | loop fusion | bytes 393232 | tf_op jit(solution)/shard_map/jit(dynamic_index_in_dim)/dynamic_slice | solution.py:73
  57.3 7.2 %multiply_convert_fusion.3 = (bf16[384,1024]{1,0:T(8,128)(2,1)S(1)}, f32[384,1024]{1,0:T(8,128)S(1)}) fusion(bf16[384,4096]{1,0:T(8,128)(2,1)} %bitcast.100, bf16[1,4096,2048]{2,1,0:T(8,128)(2,1)} %param.6, s32[]{:T(128)S(6)} %select_n.136), kind=kOutput, calls=%fused_computation.51 | convolution fusion | flops 3223191552 | bytes 13893636 | tf_op jit(solution)/shard_map/dot_general | solution.py:69
  64.5 12.2 %collective-permute-done.9 = bf16[2,4,2,24,1024]{4,3,2,1,0:T(8,128)(2,1)S(1)} collective-permute-done((bf16[2,4,2,24,1024]{4,3,2,1,0:T(8,128)(2,1)}, bf16[2,4,2,24,1024]{4,3,2,1,0:T(8,128)(2,1)S(1)}, u32[]{:S(2)}, u32[]{:S(2)}) %collective-permute-start.9) | collective-permute-done | bytes 786464 | tf_op jit(solution)/shard_map/ppermute | solution.py:30
  85.3 5.5 %multiply_convert_fusion = (bf16[384,1024]{1,0:T(8,128)(2,1)S(1)}, f32[384,1024]{1,0:T(8,128)S(1)}) fusion(bf16[384,4096]{1,0:T(8,128)(2,1)} %collective-permute-done.10, bf16[1,4096,2048]{2,1,0:T(8,128)(2,1)S(1)} %bitcast.121, s32[]{:T(128)S(6)} %select_n.136), kind=kOutput, calls=%fused_computation.47 | convolution fusion | flops 3223191552 | bytes 13893636 | tf_op jit(solution)/shard_map/dot_general | solution.py:69
  93.1 7.7 %collective-permute-done.12 = bf16[384,1024]{1,0:T(8,128)(2,1)S(1)} collective-permute-done((bf16[384,1024]{1,0:T(8,128)(2,1)S(1)}, bf16[384,1024]{1,0:T(8,128)(2,1)S(1)}, u32[]{:S(2)}, u32[]{:S(2)}) %collective-permute-start.12) | collective-permute-done | bytes 786464 | tf_op jit(solution)/shard_map/ppermute | solution.py:30
  102.2 6.0 %fusion.10 = bf16[384,4096]{1,0:T(8,128)(2,1)} fusion(bf16[384,1024]{1,0:T(8,128)(2,1)} %multiply_convert_fusion.1, bf16[1,4096,2048]{2,1,0:T(8,128)(2,1)S(1)} %bitcast.121, s32[]{:T(128)S(6)} %select_n.136), kind=kOutput, calls=%fused_computation.9 | convolution fusion | flops 3222798336 | bytes 12320772 | tf_op jit(solution)/shard_map/dot_general | solution.py:69
  112.0 7.7 %all-to-all-start.2 = ((bf16[16,4,24,1024]{3,2,1,0:T(8,128)(2,1)}), bf16[16,4,24,1024]{3,2,1,0:T(8,128)(2,1)}, u32[]{:S(2)}, u32[]{:S(2)}) async-start(bf16[16,4,24,1024]{3,2,1,0:T(8,128)(2,1)} %broadcast_in_dim.4), calls=%async_computation.2 | async-start | bytes 6291456 | tf_op jit(solution)/shard_map/all_to_all | solution.py:65
  124.8 10.9 %add_convert_fusion = bf16[384,4096]{1,0:T(8,128)(2,1)} fusion(bf16[384,4096]{1,0:T(8,128)(2,1)} %collective-permute-done.13, bf16[384,1024]{1,0:T(8,128)(2,1)S(1)} %copy-done.12, bf16[1,4096,2048]{2,1,0:T(8,128)(2,1)} %param.6, s32[]{:T(128)S(6)} %select_n.136), kind=kOutput, calls=%fused_computation.8 | convolution fusion | flops 3225944064 | bytes 15466500 | tf_op jit(solution)/shard_map/dot_general | solution.py:69
  135.7 43.2 %all-to-all-done.2 = bf16[16,4,24,1024]{3,2,1,0:T(8,128)(2,1)} async-done(((bf16[16,4,24,1024]{3,2,1,0:T(8,128)(2,1)}), bf16[16,4,24,1024]{3,2,1,0:T(8,128)(2,1)}, u32[]{:S(2)}, u32[]{:S(2)}) %all-to-all-start.2) | async-done | bytes 3145760 | tf_op jit(solution)/shard_map/all_to_all | solution.py:65
  178.9 4.0 %copy.65 = bf16[16,4,24,1024]{3,2,0,1:T(8,128)(2,1)} copy(bf16[16,4,24,1024]{3,2,1,0:T(8,128)(2,1)} %all-to-all-done.2) | data formatting | bytes 6291456 | tf_op jit(solution)/shard_map/optimization_barrier | solution.py:171
  192.0 5.6 %all-to-all-start.3 = ((bf16[16,24,1024]{2,1,0:T(8,128)(2,1)}), bf16[16,24,1024]{2,1,0:T(8,128)(2,1)S(1)}, u32[]{:S(2)}, u32[]{:S(2)}) async-start(bf16[16,24,1024]{2,1,0:T(8,128)(2,1)} %bitcast.24), calls=%async_computation.3 | async-start | bytes 1572864 | tf_op jit(solution)/shard_map/all_to_all | solution.py:177
  197.6 4.3 %convolution_convert_fusion = bf16[1024,1024]{1,0:T(8,128)(2,1)} fusion(bf16[768,1024]{1,0:T(8,128)(2,1)S(1)} %bitcast.106, bf16[384,1024]{1,0:T(8,128)(2,1)} %copy-done.7, bf16[384,1024]{1,0:T(8,128)(2,1)S(1)} %copy-done.6), kind=kOutput, calls=%fused_computation.39 | convolution fusion | flops 1614807040 | bytes 5242880 | tf_op jit(solution)/shard_map/dot_general | solution.py:69
  204.1 3.3 %slice.42 = bf16[3,16,24,1024]{3,2,1,0:T(8,128)(2,1)} slice(bf16[4,16,24,1024]{3,2,1,0:T(8,128)(2,1)} %bitcast.77.clone.2), slice={[0:3], [0:16], [0:24], [0:1024]} | slice | bytes 4718592 | tf_op jit(solution)/shard_map/slice | solution.py:199
  207.5 4.5 %all-to-all-done.3 = bf16[16,24,1024]{2,1,0:T(8,128)(2,1)S(1)} async-done(((bf16[16,24,1024]{2,1,0:T(8,128)(2,1)}), bf16[16,24,1024]{2,1,0:T(8,128)(2,1)S(1)}, u32[]{:S(2)}, u32[]{:S(2)}) %all-to-all-start.3) | async-done | bytes 786464 | tf_op jit(solution)/shard_map/all_to_all | solution.py:177
  213.0 3.6 %all-to-all-start.4 = ((bf16[16,24,4096]{2,1,0:T(8,128)(2,1)}), bf16[16,24,4096]{2,1,0:T(8,128)(2,1)S(1)}, u32[]{:S(2)}, u32[]{:S(2)}) async-start(bf16[16,24,4096]{2,1,0:T(8,128)(2,1)} %bitcast.104), calls=%async_computation.4 | async-start | bytes 6291456 | tf_op jit(solution)/shard_map/all_to_all | solution.py:65
  216.6 5.3 %fusion.19 = f32[1024,1024]{1,0:T(8,128)S(1)} fusion(bf16[1152,1024]{1,0:T(8,128)(2,1)} %bitcast.105, bf16[384,1024]{1,0:T(8,128)(2,1)} %copy-done.14, bf16[384,1024]{1,0:T(8,128)(2,1)} %collective-permute-done.11, bf16[384,1024]{1,0:T(8,128)(2,1)} %copy-done.11), kind=kOutput, calls=%fused_computation.18 | convolution fusion | flops 2422996992 | bytes 8912896 | tf_op jit(solution)/shard_map/dot_general | solution.py:69
  224.5 5.1 %fusion.17 = f32[1024,1024]{1,0:T(8,128)S(1)} fusion(bf16[1536,1024]{1,0:T(8,128)(2,1)} %collective-permute-done.18, bf16[384,1024]{1,0:T(8,128)(2,1)} %collective-permute-done.15, bf16[384,1024]{1,0:T(8,128)(2,1)} %collective-permute-done.14, bf16[384,1024]{1,0:T(8,128)(2,1)S(1)} %copy-done.13), kind=kOutput, calls=%fused_computation.16 | convolution fusion | flops 2422996992 | bytes 8912896 | tf_op jit(solution)/shard_map/dot_general | solution.py:69
  229.6 10.1 %collective-permute-done.19 = bf16[384,1024]{1,0:T(8,128)(2,1)} collective-permute-done((bf16[384,1024]{1,0:T(8,128)(2,1)}, bf16[384,1024]{1,0:T(8,128)(2,1)}, u32[]{:S(2)}, u32[]{:S(2)}) %collective-permute-start.19) | collective-permute-done | bytes 786464 | tf_op jit(solution)/shard_map/ppermute | solution.py:30
  248.1 26.4 %all-to-all-done.4 = bf16[16,24,4096]{2,1,0:T(8,128)(2,1)S(1)} async-done(((bf16[16,24,4096]{2,1,0:T(8,128)(2,1)}), bf16[16,24,4096]{2,1,0:T(8,128)(2,1)S(1)}, u32[]{:S(2)}, u32[]{:S(2)}) %all-to-all-start.4) | async-done | bytes 3145760 | tf_op jit(solution)/shard_map/all_to_all | solution.py:65
  275.9 7.7 %all-to-all-start.5 = ((bf16[16,8,24]{2,1,0:T(8,128)(2,1)}), bf16[16,8,24]{2,1,0:T(8,128)(2,1)}, u32[]{:S(2)}, u32[]{:S(2)}) async-start(bf16[16,8,24]{2,1,0:T(8,128)(2,1)} %copy.48), calls=%async_computation.5 | async-start | bytes 65536 | tf_op jit(solution)/shard_map/all_to_all | solution.py:196
  287.3 3.8 %all-to-all-done.5 = bf16[16,8,24]{2,1,0:T(8,128)(2,1)} async-done(((bf16[16,8,24]{2,1,0:T(8,128)(2,1)}), bf16[16,8,24]{2,1,0:T(8,128)(2,1)}, u32[]{:S(2)}, u32[]{:S(2)}) %all-to-all-start.5) | async-done | bytes 6176 | tf_op jit(solution)/shard_map/all_to_all | solution.py:196
  292.5 4.5 %maximum_select_fusion = bf16[1,512,2048]{2,1,0:T(8,128)(2,1)} fusion(bf16[1,512,1024]{2,1,0:T(8,128)(2,1)} %bitcast.35, bf16[1,512,1024]{2,1,0:T(8,128)(2,1)} %get-tuple-element.55, pred[]{:T(512)S(6)} %eq.17), kind=kLoop, calls=%fused_computation.29 | loop fusion | flops 9437184 | bytes 4194305 | tf_op jit(solution)/shard_map/jit(_where)/select_n | solution.py:206
  (123 shorter events, 84.2 us)
Async XLA Ops:
  7.2 13.6 %collective-permute-start.1 = (bf16[24,4096]{1,0:T(8,128)(2,1)}, bf16[24,4096]{1,0:T(8,128)(2,1)S(1)}, u32[]{:S(2)}, u32[]{:S(2)}) collective-permute-start(bf16[24,4096]{1,0:T(8,128)(2,1)} %param.5), channel_id=1, source_target_pairs={{0,4},{1,5},{2,6},{3,7},{4,0},{5,1},{6,2},{7,3},{8,40},{9,41},{10,... | collective-permute-start | bytes 589832 | tf_op jit(solution)/shard_map/ppermute | solution.py:42
  10.0 10.8 %collective-permute-start = (bf16[24,4096]{1,0:T(8,128)(2,1)}, bf16[24,4096]{1,0:T(8,128)(2,1)S(1)}, u32[]{:S(2)}, u32[]{:S(2)}) collective-permute-start(bf16[24,4096]{1,0:T(8,128)(2,1)} %param.5), channel_id=1, source_target_pairs={{0,64},{1,65},{2,66},{3,67},{4,68},{5,69},{6,70},{7,71},{8,24},{9,... | collective-permute-start | bytes 589832 | tf_op jit(solution)/shard_map/ppermute | solution.py:42
  12.3 15.9 %all-to-all-start = ((bf16[16,8,24]{2,1,0:T(8,128)(2,1)}), bf16[16,8,24]{2,1,0:T(8,128)(2,1)}, u32[]{:S(2)}, u32[]{:S(2)}) async-start(bf16[16,8,24]{2,1,0:T(8,128)(2,1)} %copy.35), calls=%async_computation | async-start | bytes 65536 | tf_op jit(solution)/shard_map/all_to_all | solution.py:105
  21.8 30.9 %collective-permute-start.5 = (bf16[4,24,4096]{2,1,0:T(8,128)(2,1)S(1)}, bf16[4,24,4096]{2,1,0:T(8,128)(2,1)S(1)}, u32[]{:S(2)}, u32[]{:S(2)}) collective-permute-start(bf16[4,24,4096]{2,1,0:T(8,128)(2,1)S(1)} %pad_maximum_fusion.1.refs_0_), channel_id=1, source_target_pairs={{0,48},{1,49},{2,50},{3,51},{4,52},{5,53},{6,54},{7,55},{8,76},{9,... | collective-permute-start | bytes 2359304 | tf_op jit(solution)/shard_map/ppermute | solution.py:42
  22.5 30.2 %collective-permute-start.4 = (bf16[4,24,4096]{2,1,0:T(8,128)(2,1)S(1)}, bf16[4,24,4096]{2,1,0:T(8,128)(2,1)S(1)}, u32[]{:S(2)}, u32[]{:S(2)}) collective-permute-start(bf16[4,24,4096]{2,1,0:T(8,128)(2,1)S(1)} %pad_maximum_fusion.1.refs_0_), channel_id=1, source_target_pairs={{0,32},{1,33},{2,34},{3,35},{4,36},{5,37},{6,38},{7,39},{8,12},{9,... | collective-permute-start | bytes 2359304 | tf_op jit(solution)/shard_map/ppermute | solution.py:42
  25.7 27.1 %collective-permute-start.3 = (bf16[4,24,4096]{2,1,0:T(8,128)(2,1)S(1)}, bf16[4,24,4096]{2,1,0:T(8,128)(2,1)S(1)}, u32[]{:S(2)}, u32[]{:S(2)}) collective-permute-start(bf16[4,24,4096]{2,1,0:T(8,128)(2,1)S(1)} %pad_maximum_fusion.1.refs_0_), channel_id=1, source_target_pairs={{0,16},{1,17},{2,18},{3,19},{4,20},{5,21},{6,22},{7,23},{8,72},{9,... | collective-permute-start | bytes 2359304 | tf_op jit(solution)/shard_map/ppermute | solution.py:42
  32.2 23.6 %all-to-all-start.1 = ((bf16[16,24,1024]{2,1,0:T(8,128)(2,1)}), bf16[16,24,1024]{2,1,0:T(8,128)(2,1)}, u32[]{:S(2)}, u32[]{:S(2)}) async-start(bf16[16,24,1024]{2,1,0:T(8,128)(2,1)} %copy.37), calls=%async_computation.1 | async-start | bytes 1572864 | tf_op jit(solution)/shard_map/all_to_all | solution.py:120
  55.8 26.5 %collective-permute-start.10 = (bf16[384,4096]{1,0:T(8,128)(2,1)}, bf16[384,4096]{1,0:T(8,128)(2,1)}, u32[]{:S(2)}, u32[]{:S(2)}) collective-permute-start(bf16[384,4096]{1,0:T(8,128)(2,1)} %bitcast.99), channel_id=1, source_target_pairs={{0,8},{1,9},{2,10},{3,11},{4,12},{5,13},{6,14},{7,15},{8,0},{9,1},... | collective-permute-start | bytes 9437192 | tf_op jit(solution)/shard_map/ppermute | solution.py:30
  57.3 19.4 %collective-permute-start.9 = (bf16[2,4,2,24,1024]{4,3,2,1,0:T(8,128)(2,1)}, bf16[2,4,2,24,1024]{4,3,2,1,0:T(8,128)(2,1)S(1)}, u32[]{:S(2)}, u32[]{:S(2)}) collective-permute-start(bf16[2,4,2,24,1024]{4,3,2,1,0:T(8,128)(2,1)} %bitcast.12), channel_id=1, source_target_pairs={{0,4},{1,5},{2,6},{3,7},{4,0},{5,1},{6,2},{7,3},{8,12},{9,13},{10,... | collective-permute-start | bytes 2359304 | tf_op jit(solution)/shard_map/ppermute | solution.py:30
  82.3 18.5 %collective-permute-start.12 = (bf16[384,1024]{1,0:T(8,128)(2,1)S(1)}, bf16[384,1024]{1,0:T(8,128)(2,1)S(1)}, u32[]{:S(2)}, u32[]{:S(2)}) collective-permute-start(bf16[384,1024]{1,0:T(8,128)(2,1)S(1)} %multiply_convert_fusion.2), channel_id=1, source_target_pairs={{0,3},{1,2},{2,1},{3,0},{4,7},{5,6},{6,5},{7,4},{8,11},{9,10},{10,... | collective-permute-start | bytes 2359304 | tf_op jit(solution)/shard_map/ppermute | solution.py:30
  83.1 19.1 %collective-permute-start.11 = (bf16[384,1024]{1,0:T(8,128)(2,1)S(1)}, bf16[384,1024]{1,0:T(8,128)(2,1)}, u32[]{:S(2)}, u32[]{:S(2)}) collective-permute-start(bf16[384,1024]{1,0:T(8,128)(2,1)S(1)} %multiply_convert_fusion.2), channel_id=1, source_target_pairs={{0,1},{1,0},{2,3},{3,2},{4,5},{5,4},{6,7},{7,6},{8,9},{9,8},{10,11... | collective-permute-start | bytes 2359304 | tf_op jit(solution)/shard_map/ppermute | solution.py:30
  108.2 16.6 %collective-permute-start.13 = (bf16[384,4096]{1,0:T(8,128)(2,1)}, bf16[384,4096]{1,0:T(8,128)(2,1)}, u32[]{:S(2)}, u32[]{:S(2)}) collective-permute-start(bf16[384,4096]{1,0:T(8,128)(2,1)} %fusion.10), channel_id=1, source_target_pairs={{0,8},{1,9},{2,10},{3,11},{4,12},{5,13},{6,14},{7,15},{8,0},{9,1},... | collective-permute-start | bytes 9437192 | tf_op jit(solution)/shard_map/ppermute | solution.py:30
  112.0 66.8 %all-to-all-start.2 = ((bf16[16,4,24,1024]{3,2,1,0:T(8,128)(2,1)}), bf16[16,4,24,1024]{3,2,1,0:T(8,128)(2,1)}, u32[]{:S(2)}, u32[]{:S(2)}) async-start(bf16[16,4,24,1024]{3,2,1,0:T(8,128)(2,1)} %broadcast_in_dim.4), calls=%async_computation.2 | async-start | bytes 6291456 | tf_op jit(solution)/shard_map/all_to_all | solution.py:65
  119.7 59.2 %collective-permute-start.15 = (bf16[384,1024]{1,0:T(8,128)(2,1)}, bf16[384,1024]{1,0:T(8,128)(2,1)}, u32[]{:S(2)}, u32[]{:S(2)}) collective-permute-start(bf16[384,1024]{1,0:T(8,128)(2,1)} %multiply_convert_fusion.1), channel_id=1, source_target_pairs={{0,3},{1,2},{2,1},{3,0},{4,7},{5,6},{6,5},{7,4},{8,11},{9,10},{10,... | collective-permute-start | bytes 2359304 | tf_op jit(solution)/shard_map/ppermute | solution.py:30
  121.0 57.9 %collective-permute-start.14 = (bf16[384,1024]{1,0:T(8,128)(2,1)}, bf16[384,1024]{1,0:T(8,128)(2,1)}, u32[]{:S(2)}, u32[]{:S(2)}) collective-permute-start(bf16[384,1024]{1,0:T(8,128)(2,1)} %multiply_convert_fusion.1), channel_id=1, source_target_pairs={{0,1},{1,0},{2,3},{3,2},{4,5},{5,4},{6,7},{7,6},{8,9},{9,8},{10,11... | collective-permute-start | bytes 2359304 | tf_op jit(solution)/shard_map/ppermute | solution.py:30
  124.6 62.4 %collective-permute-start.16 = (bf16[384,1024]{1,0:T(8,128)(2,1)}, bf16[384,1024]{1,0:T(8,128)(2,1)}, u32[]{:S(2)}, u32[]{:S(2)}) collective-permute-start(bf16[384,1024]{1,0:T(8,128)(2,1)} %bitcast.20), channel_id=1, source_target_pairs={{0,4},{1,5},{2,6},{3,7},{4,0},{5,1},{6,2},{7,3},{8,12},{9,13},{10,... | collective-permute-start | bytes 2359304 | tf_op jit(solution)/shard_map/ppermute | solution.py:30
  182.9 41.6 %collective-permute-start.18 = (bf16[1536,1024]{1,0:T(8,128)(2,1)}, bf16[1536,1024]{1,0:T(8,128)(2,1)}, u32[]{:S(2)}, u32[]{:S(2)}) collective-permute-start(bf16[1536,1024]{1,0:T(8,128)(2,1)} %bitcast.31), channel_id=1, source_target_pairs={{0,8},{1,9},{2,10},{3,11},{4,12},{5,13},{6,14},{7,15},{8,0},{9,1},... | collective-permute-start | bytes 9437192 | tf_op jit(solution)/shard_map/ppermute | solution.py:30
  184.2 23.3 %collective-permute-start.17 = (bf16[384,1024]{1,0:T(8,128)(2,1)}, bf16[384,1024]{1,0:T(8,128)(2,1)}, u32[]{:S(2)}, u32[]{:S(2)}) collective-permute-start(bf16[384,1024]{1,0:T(8,128)(2,1)} %copy-done.14), channel_id=1, source_target_pairs={{0,1},{1,0},{2,3},{3,2},{4,5},{5,4},{6,7},{7,6},{8,9},{9,8},{10,11... | collective-permute-start | bytes 2359304 | tf_op jit(solution)/shard_map/ppermute | solution.py:30
  192.0 20.1 %all-to-all-start.3 = ((bf16[16,24,1024]{2,1,0:T(8,128)(2,1)}), bf16[16,24,1024]{2,1,0:T(8,128)(2,1)S(1)}, u32[]{:S(2)}, u32[]{:S(2)}) async-start(bf16[16,24,1024]{2,1,0:T(8,128)(2,1)} %bitcast.24), calls=%async_computation.3 | async-start | bytes 1572864 | tf_op jit(solution)/shard_map/all_to_all | solution.py:177
  197.6 99.4 %reduce-scatter.2.cloned.1.call-start = ((), (), s32[]{:S(2)}) async-start(), calls=%async_computation.7 | async-start | bytes 2621440 | tf_op jit(solution)/shard_map/reduce_scatter | solution.py:185
  207.4 32.3 %collective-permute-start.19 = (bf16[384,1024]{1,0:T(8,128)(2,1)}, bf16[384,1024]{1,0:T(8,128)(2,1)}, u32[]{:S(2)}, u32[]{:S(2)}) collective-permute-start(bf16[384,1024]{1,0:T(8,128)(2,1)} %collective-permute-done.14), channel_id=1, source_target_pairs={{0,3},{1,2},{2,1},{3,0},{4,7},{5,6},{6,5},{7,4},{8,11},{9,10},{10,... | collective-permute-start | bytes 2359304 | tf_op jit(solution)/shard_map/ppermute | solution.py:30
  213.0 61.5 %all-to-all-start.4 = ((bf16[16,24,4096]{2,1,0:T(8,128)(2,1)}), bf16[16,24,4096]{2,1,0:T(8,128)(2,1)S(1)}, u32[]{:S(2)}, u32[]{:S(2)}) async-start(bf16[16,24,4096]{2,1,0:T(8,128)(2,1)} %bitcast.104), calls=%async_computation.4 | async-start | bytes 6291456 | tf_op jit(solution)/shard_map/all_to_all | solution.py:65
  244.3 48.2 %collective-permute-start.20 = (bf16[512,1024]{1,0:T(8,128)(2,1)}, bf16[512,1024]{1,0:T(8,128)(2,1)}, u32[]{:S(2)}, u32[]{:S(2)}) collective-permute-start(bf16[512,1024]{1,0:T(8,128)(2,1)} %get-tuple-element.56), channel_id=1, source_target_pairs={{0,4},{1,5},{2,6},{3,7},{4,0},{5,1},{6,2},{7,3},{8,12},{9,13},{10,... | collective-permute-start | bytes 3145736 | tf_op jit(solution)/shard_map/ppermute | solution.py:30
  275.9 15.1 %all-to-all-start.5 = ((bf16[16,8,24]{2,1,0:T(8,128)(2,1)}), bf16[16,8,24]{2,1,0:T(8,128)(2,1)}, u32[]{:S(2)}, u32[]{:S(2)}) async-start(bf16[16,8,24]{2,1,0:T(8,128)(2,1)} %copy.48), calls=%async_computation.5 | async-start | bytes 65536 | tf_op jit(solution)/shard_map/all_to_all | solution.py:196
  (23 other events, 285.8 us)
Sparse Core Ops, SparseCore 0:
  202.1 42.9 reduce-scatter.1
where the time goes:
time: 305 us; the launch traced here: 304 us
  waiting for transfers between devices  112 us (37%)
  matrix products  63.1 us (21%)
  starting transfers between devices  62.9 us (21%)
  local copies, waits for them, and re-layouts  39.5 us (13%)
  between operations  14.4 us (5%)
  other arithmetic  10.7 us (4%)
    all_to_all x2, waiting for transfers between devices, exchange(): return lax.all_to_all(v, AXES, 0, 0, axis_index_groups=members, tiled=True)  69.6 us
    dot_general x13, matrix products, dot(): return lax.dot_general(a, b, (dims, ((), ())), preferred_element_type=F32)  57.2 us
    ppermute x15, waiting for transfers between devices, swap(): return lax.ppermute(v, AXES, pairs)  31.4 us
    ppermute x15, starting transfers between devices, swap(): return lax.ppermute(v, AXES, pairs)  17.3 us
    all_to_all x2, starting transfers between devices, exchange(): return lax.all_to_all(v, AXES, 0, 0, axis_index_groups=members, tiled=True)  11.3 us
    unnamed x41, local copies, waits for them, and re-layouts  8.87 us
    all_to_all x1, starting transfers between devices, on_device(): lax.all_to_all(gates[0].reshape(8, 16, 24).transpose(1, 0, 2), 'expert',...  8.49 us
    all_to_all x1, starting transfers between devices, on_device(): d_gate = lax.all_to_all(after(d_gate, dt), 'expert', 0, 0, tiled=True)  7.67 us
  transfers between devices with their start and end apart: 28, of which 11 were waited for; matrix products, arithmetic and copies ran while one was open for 34% of the time, Pallas kernels for 0%

commit v1 on v0

--- a/solution.py
+++ b/solution.py
@@ -165,16 +165,18 @@
     d_late, near_own = lax.optimization_barrier((d_other, near_own))
     far_own = swap(near_own[1], y=1)
     dt_other = dot(d_late, half, ((1,), (1,))).astype(BF)
-    dt = dot(d_own, half, ((1,), (1,))) + swap(dt_other, c=1).astype(F32)
-    dt = dt.astype(BF)
-
-    dt, mine, near_other, wide = lax.optimization_barrier((dt, mine, near_other, wide))
+
+    mine, theirs, near_other, wide, dt_other = lax.optimization_barrier(
+        (mine, theirs, near_other, wide, dt_other)
+    )
     far_other = swap(near_other[0], y=3)
     output = dot(mine, second_own, ((1,), (0,))) + dot(theirs, second_far, ((1,), (0,)))
     output = output.astype(BF).reshape(2, 4, 2, 24, 1024)
     output = jnp.where(c == 0, output, output[::-1])
     output = output.transpose(2, 1, 0, 3, 4).reshape(16, 24, 1024)
     outs = lax.all_to_all(output, "expert", 0, 0, tiled=True)
+    dt = dot(after(d_own, output), half, ((1,), (1,))) + swap(dt_other, c=1).astype(F32)
+    dt = dt.astype(BF)
     dt, outs, far_own = lax.optimization_barrier((dt, outs, far_own))
     dt = exchange(dt.reshape(16, 24, 4096), PLANE)
     d_trunk = jnp.sum(dt, axis=0, dtype=F32).astype(BF)

time: 305 us -> 288 us (0.944)
  the two profiles are of different devices: /device:TPU:49 before, /device:TPU:1 now
where the time goes in v1:
time: 288 us; the launch traced here: 284 us
  waiting for transfers between devices  79.9 us (28%)
  starting transfers between devices  74.4 us (26%)
  matrix products  58.5 us (20%)
  local copies, waits for them, and re-layouts  40.3 us (14%)
  other arithmetic  15.3 us (5%)
  between operations  14.4 us (5%)
    dot_general x13, matrix products, dot(): return lax.dot_general(a, b, (dims, ((), ())), preferred_element_type=F32)  52.6 us
    all_to_all x2, waiting for transfers between devices, exchange(): return lax.all_to_all(v, AXES, 0, 0, axis_index_groups=members, tiled=True)  43 us
    ppermute x15, waiting for transfers between devices, swap(): return lax.ppermute(v, AXES, pairs)  33.3 us
    ppermute x15, starting transfers between devices, swap(): return lax.ppermute(v, AXES, pairs)  17.3 us
    all_to_all x2, starting transfers between devices, exchange(): return lax.all_to_all(v, AXES, 0, 0, axis_index_groups=members, tiled=True)  13.8 us
    all_to_all x1, starting transfers between devices, on_device(): outs = lax.all_to_all(output, 'expert', 0, 0, tiled=True)  13.4 us
    unnamed x39, local copies, waits for them, and re-layouts  10.5 us
    all_to_all x1, starting transfers between devices, on_device(): lax.all_to_all(gates[0].reshape(8, 16, 24).transpose(1, 0, 2), 'expert',...  8.84 us
  transfers between devices with their start and end apart: 28, of which 12 were waited for; matrix products, arithmetic and copies ran while one was open for 38% of the time, Pallas kernels for 0%

profile of v1, /device:TPU:1, one launch (start us, length us, event | category | flops | bytes accessed | tf_op | source)
XLA Modules:
  0.0 283.6 jit_solution(14528794732115701426)
XLA Ops:
  7.2 3.4 %collective-permute-start.2 = (bf16[24,4096]{1,0:T(8,128)(2,1)}, bf16[24,4096]{1,0:T(8,128)(2,1)S(1)}, u32[]{:S(2)}, u32[]{:S(2)}) collective-permute-start(bf16[24,4096]{1,0:T(8,128)(2,1)} %param.5), channel_id=1, source_target_pairs={{0,68},{1,69},{2,70},{3,71},{4,64},{5,65},{6,66},{7,67},{8,56},{9,... | collective-permute-start | bytes 589832 | tf_op jit(solution)/shard_map/ppermute | solution.py:42
  12.7 8.8 %all-to-all-start = ((bf16[16,8,24]{2,1,0:T(8,128)(2,1)}), bf16[16,8,24]{2,1,0:T(8,128)(2,1)}, u32[]{:S(2)}, u32[]{:S(2)}) async-start(bf16[16,8,24]{2,1,0:T(8,128)(2,1)} %copy.35), calls=%async_computation | async-start | bytes 65536 | tf_op jit(solution)/shard_map/all_to_all | solution.py:105
  32.9 5.4 %all-to-all-start.1 = ((bf16[16,24,1024]{2,1,0:T(8,128)(2,1)}), bf16[16,24,1024]{2,1,0:T(8,128)(2,1)}, u32[]{:S(2)}, u32[]{:S(2)}) async-start(bf16[16,24,1024]{2,1,0:T(8,128)(2,1)} %copy.37), calls=%async_computation.1 | async-start | bytes 1572864 | tf_op jit(solution)/shard_map/all_to_all | solution.py:120
  40.0 3.2 %dynamic-slice_reduce_fusion.3 = (bf16[24,2,512]{2,1,0:T(2,128)(2,1)}, bf16[24,2,512]{2,1,0:T(2,128)(2,1)}, bf16[24,2,512]{2,1,0:T(2,128)(2,1)}, bf16[24,2,512]{2,1,0:T(2,128)(2,1)S(1)}) fusion(bf16[24,2,4,512]{3,2,1,0:T(4,128)(2,1)} %reshape.121, s32[]{:T(128)S(6)} %select_n.132, s32[]{:T(128)S(6)} %select_n.134, s32[]{:T(128)S(6)} %select_n.133, ...), kind=kLoop, calls=%fused_computation.71 | loop fusion | bytes 393232 | tf_op jit(solution)/shard_map/jit(dynamic_index_in_dim)/dynamic_slice | solution.py:73
  61.7 9.0 %multiply_convert_fusion.3 = (bf16[384,1024]{1,0:T(8,128)(2,1)S(1)}, f32[384,1024]{1,0:T(8,128)}) fusion(bf16[384,4096]{1,0:T(8,128)(2,1)} %bitcast.98, bf16[1,4096,2048]{2,1,0:T(8,128)(2,1)} %param.6, s32[]{:T(128)S(6)} %select_n.136), kind=kOutput, calls=%fused_computation.51 | convolution fusion | flops 3223191552 | bytes 13893636 | tf_op jit(solution)/shard_map/dot_general | solution.py:69
  70.6 9.2 %collective-permute-done.9 = bf16[2,4,2,24,1024]{4,3,2,1,0:T(8,128)(2,1)S(1)} collective-permute-done((bf16[2,4,2,24,1024]{4,3,2,1,0:T(8,128)(2,1)}, bf16[2,4,2,24,1024]{4,3,2,1,0:T(8,128)(2,1)S(1)}, u32[]{:S(2)}, u32[]{:S(2)}) %collective-permute-start.9) | collective-permute-done | bytes 786464 | tf_op jit(solution)/shard_map/ppermute | solution.py:30
  81.9 7.2 %all-to-all-start.2 = ((bf16[16,4,24,1024]{3,2,1,0:T(8,128)(2,1)}), bf16[16,4,24,1024]{3,2,1,0:T(8,128)(2,1)}, u32[]{:S(2)}, u32[]{:S(2)}) async-start(bf16[16,4,24,1024]{3,2,1,0:T(8,128)(2,1)} %broadcast_in_dim.4), calls=%async_computation.2 | async-start | bytes 6291456 | tf_op jit(solution)/shard_map/all_to_all | solution.py:65
  97.6 7.2 %multiply_convert_fusion.1 = (bf16[384,1024]{1,0:T(8,128)(2,1)S(1)}, f32[384,1024]{1,0:T(8,128)S(1)}) fusion(bf16[384,4096]{1,0:T(8,128)(2,1)} %collective-permute-done.10, bf16[1,4096,2048]{2,1,0:T(8,128)(2,1)} %param.6, s32[]{:T(128)S(6)} %select_n.136), kind=kOutput, calls=%fused_computation.48 | convolution fusion | flops 3223191552 | bytes 13893636 | tf_op jit(solution)/shard_map/dot_general | solution.py:69
  114.5 6.1 %fusion.8 = bf16[384,4096]{1,0:T(8,128)(2,1)} fusion(bf16[384,1024]{1,0:T(8,128)(2,1)} %multiply_convert_fusion, bf16[1,4096,2048]{2,1,0:T(8,128)(2,1)S(1)} %bitcast.119, s32[]{:T(128)S(6)} %select_n.136), kind=kOutput, calls=%fused_computation.9 | convolution fusion | flops 3222798336 | bytes 12320772 | tf_op jit(solution)/shard_map/dot_general | solution.py:69
  120.6 14.9 %all-to-all-done.2 = bf16[16,4,24,1024]{3,2,1,0:T(8,128)(2,1)} async-done(((bf16[16,4,24,1024]{3,2,1,0:T(8,128)(2,1)}), bf16[16,4,24,1024]{3,2,1,0:T(8,128)(2,1)}, u32[]{:S(2)}, u32[]{:S(2)}) %all-to-all-start.2) | async-done | bytes 3145760 | tf_op jit(solution)/shard_map/all_to_all | solution.py:65
  135.5 5.8 %collective-permute-done.11 = bf16[384,1024]{1,0:T(8,128)(2,1)} collective-permute-done((bf16[384,1024]{1,0:T(8,128)(2,1)}, bf16[384,1024]{1,0:T(8,128)(2,1)}, u32[]{:S(2)}, u32[]{:S(2)}) %collective-permute-start.11) | collective-permute-done | bytes 786464 | tf_op jit(solution)/shard_map/ppermute | solution.py:30
  144.2 3.2 %convolution_convert_fusion = bf16[1024,1024]{1,0:T(8,128)(2,1)} fusion(bf16[768,1024]{1,0:T(8,128)(2,1)S(1)} %bitcast.104, bf16[384,1024]{1,0:T(8,128)(2,1)S(1)} %copy-done.5, bf16[384,1024]{1,0:T(8,128)(2,1)S(1)} %get-tuple-element.36), kind=kOutput, calls=%fused_computation.39 | convolution fusion | flops 1614807040 | bytes 5242880 | tf_op jit(solution)/shard_map/dot_general | solution.py:69
  147.4 4.2 %copy.65 = bf16[16,4,24,1024]{3,2,0,1:T(8,128)(2,1)} copy(bf16[16,4,24,1024]{3,2,1,0:T(8,128)(2,1)} %all-to-all-done.2) | data formatting | bytes 6291456 | tf_op jit(solution)/shard_map/optimization_barrier | solution.py:169
  155.8 13.4 %all-to-all-start.3 = ((bf16[16,24,1024]{2,1,0:T(8,128)(2,1)}), bf16[16,24,1024]{2,1,0:T(8,128)(2,1)S(1)}, u32[]{:S(2)}, u32[]{:S(2)}) async-start(bf16[16,24,1024]{2,1,0:T(8,128)(2,1)} %bitcast.24), calls=%async_computation.3 | async-start | bytes 1572864 | tf_op jit(solution)/shard_map/all_to_all | solution.py:177
  169.4 3.4 %slice.42 = bf16[3,16,24,1024]{3,2,1,0:T(8,128)(2,1)} slice(bf16[4,16,24,1024]{3,2,1,0:T(8,128)(2,1)} %bitcast.75.clone.2), slice={[0:3], [0:16], [0:24], [0:1024]} | slice | bytes 4718592 | tf_op jit(solution)/shard_map/slice | solution.py:201
  174.8 5.9 %fusion = f32[384,4096]{1,0:T(8,128)S(1)} fusion(bf16[384,1024]{1,0:T(8,128)(2,1)S(1)} %copy-done.11, bf16[1,4096,2048]{2,1,0:T(8,128)(2,1)} %param.6, s32[]{:T(128)S(6)} %select_n.136), kind=kOutput, calls=%fused_computation | convolution fusion | flops 3221225472 | bytes 15466500 | tf_op jit(solution)/shard_map/dot_general | solution.py:69
  180.8 4.6 %add_convert_fusion = bf16[384,4096]{1,0:T(8,128)(2,1)} fusion(f32[384,4096]{1,0:T(8,128)S(1)} %fusion, bf16[384,4096]{1,0:T(8,128)(2,1)} %collective-permute-done.16), kind=kLoop, calls=%fused_computation.8 | loop fusion | flops 4718592 | bytes 12582912 | tf_op jit(solution)/shard_map/convert_element_type | solution.py:179
  185.4 13.5 %collective-permute-done.17 = bf16[384,1024]{1,0:T(8,128)(2,1)S(1)} collective-permute-done((bf16[384,1024]{1,0:T(8,128)(2,1)}, bf16[384,1024]{1,0:T(8,128)(2,1)S(1)}, u32[]{:S(2)}, u32[]{:S(2)}) %collective-permute-start.17) | collective-permute-done | bytes 786464 | tf_op jit(solution)/shard_map/ppermute | solution.py:30
  199.8 6.6 %all-to-all-start.4 = ((bf16[16,24,4096]{2,1,0:T(8,128)(2,1)}), bf16[16,24,4096]{2,1,0:T(8,128)(2,1)S(1)}, u32[]{:S(2)}, u32[]{:S(2)}) async-start(bf16[16,24,4096]{2,1,0:T(8,128)(2,1)} %bitcast.99), calls=%async_computation.4 | async-start | bytes 6291456 | tf_op jit(solution)/shard_map/all_to_all | solution.py:65
  206.5 5.3 %fusion.17 = f32[1024,1024]{1,0:T(8,128)S(1)} fusion(bf16[1152,1024]{1,0:T(8,128)(2,1)} %bitcast.103, bf16[384,1024]{1,0:T(8,128)(2,1)} %collective-permute-done.15, bf16[384,1024]{1,0:T(8,128)(2,1)} %copy-done.12, bf16[384,1024]{1,0:T(8,128)(2,1)} %copy-done.10), kind=kOutput, calls=%fused_computation.18 | convolution fusion | flops 2422996992 | bytes 8912896 | tf_op jit(solution)/shard_map/dot_general | solution.py:69
  214.2 5.2 %fusion.15 = f32[1024,1024]{1,0:T(8,128)S(1)} fusion(bf16[1536,1024]{1,0:T(8,128)(2,1)} %collective-permute-done.18, bf16[384,1024]{1,0:T(8,128)(2,1)} %collective-permute-done.13, bf16[384,1024]{1,0:T(8,128)(2,1)} %collective-permute-done.12, bf16[384,1024]{1,0:T(8,128)(2,1)} %multiply_convert_fusion), kind=kOutput, calls=%fused_computation.16 | convolution fusion | flops 2422996992 | bytes 8912896 | tf_op jit(solution)/shard_map/dot_general | solution.py:69
  231.6 28.1 %all-to-all-done.4 = bf16[16,24,4096]{2,1,0:T(8,128)(2,1)S(1)} async-done(((bf16[16,24,4096]{2,1,0:T(8,128)(2,1)}), bf16[16,24,4096]{2,1,0:T(8,128)(2,1)S(1)}, u32[]{:S(2)}, u32[]{:S(2)}) %all-to-all-start.4) | async-done | bytes 3145760 | tf_op jit(solution)/shard_map/all_to_all | solution.py:65
  261.2 6.6 %all-to-all-start.5 = ((bf16[16,8,24]{2,1,0:T(8,128)(2,1)}), bf16[16,8,24]{2,1,0:T(8,128)(2,1)}, u32[]{:S(2)}, u32[]{:S(2)}) async-start(bf16[16,8,24]{2,1,0:T(8,128)(2,1)} %copy.48), calls=%async_computation.5 | async-start | bytes 65536 | tf_op jit(solution)/shard_map/all_to_all | solution.py:198
  267.8 4.5 %maximum_select_fusion = bf16[1,512,2048]{2,1,0:T(8,128)(2,1)} fusion(bf16[1,512,1024]{2,1,0:T(8,128)(2,1)} %bitcast.35, bf16[1,512,1024]{2,1,0:T(8,128)(2,1)} %get-tuple-element.59, pred[]{:T(512)S(6)} %eq.17), kind=kLoop, calls=%fused_computation.29 | loop fusion | flops 9437184 | bytes 4194305 | tf_op jit(solution)/shard_map/jit(_where)/select_n | solution.py:208
  (122 shorter events, 84.5 us)
Async XLA Ops:
  7.2 14.3 %collective-permute-start.2 = (bf16[24,4096]{1,0:T(8,128)(2,1)}, bf16[24,4096]{1,0:T(8,128)(2,1)S(1)}, u32[]{:S(2)}, u32[]{:S(2)}) collective-permute-start(bf16[24,4096]{1,0:T(8,128)(2,1)} %param.5), channel_id=1, source_target_pairs={{0,68},{1,69},{2,70},{3,71},{4,64},{5,65},{6,66},{7,67},{8,56},{9,... | collective-permute-start | bytes 589832 | tf_op jit(solution)/shard_map/ppermute | solution.py:42
  10.6 10.9 %collective-permute-start.1 = (bf16[24,4096]{1,0:T(8,128)(2,1)}, bf16[24,4096]{1,0:T(8,128)(2,1)S(1)}, u32[]{:S(2)}, u32[]{:S(2)}) collective-permute-start(bf16[24,4096]{1,0:T(8,128)(2,1)} %param.5), channel_id=1, source_target_pairs={{0,4},{1,5},{2,6},{3,7},{4,0},{5,1},{6,2},{7,3},{8,40},{9,41},{10,... | collective-permute-start | bytes 589832 | tf_op jit(solution)/shard_map/ppermute | solution.py:42
  12.7 16.3 %all-to-all-start = ((bf16[16,8,24]{2,1,0:T(8,128)(2,1)}), bf16[16,8,24]{2,1,0:T(8,128)(2,1)}, u32[]{:S(2)}, u32[]{:S(2)}) async-start(bf16[16,8,24]{2,1,0:T(8,128)(2,1)} %copy.35), calls=%async_computation | async-start | bytes 65536 | tf_op jit(solution)/shard_map/all_to_all | solution.py:105
  22.6 32.9 %collective-permute-start.3 = (bf16[4,24,4096]{2,1,0:T(8,128)(2,1)S(1)}, bf16[4,24,4096]{2,1,0:T(8,128)(2,1)S(1)}, u32[]{:S(2)}, u32[]{:S(2)}) collective-permute-start(bf16[4,24,4096]{2,1,0:T(8,128)(2,1)S(1)} %pad_maximum_fusion.1.refs_0_), channel_id=1, source_target_pairs={{0,16},{1,17},{2,18},{3,19},{4,20},{5,21},{6,22},{7,23},{8,72},{9,... | collective-permute-start | bytes 2359304 | tf_op jit(solution)/shard_map/ppermute | solution.py:42
  25.5 29.9 %collective-permute-start.4 = (bf16[4,24,4096]{2,1,0:T(8,128)(2,1)S(1)}, bf16[4,24,4096]{2,1,0:T(8,128)(2,1)S(1)}, u32[]{:S(2)}, u32[]{:S(2)}) collective-permute-start(bf16[4,24,4096]{2,1,0:T(8,128)(2,1)S(1)} %pad_maximum_fusion.1.refs_0_), channel_id=1, source_target_pairs={{0,32},{1,33},{2,34},{3,35},{4,36},{5,37},{6,38},{7,39},{8,12},{9,... | collective-permute-start | bytes 2359304 | tf_op jit(solution)/shard_map/ppermute | solution.py:42
  27.3 28.2 %collective-permute-start.5 = (bf16[4,24,4096]{2,1,0:T(8,128)(2,1)S(1)}, bf16[4,24,4096]{2,1,0:T(8,128)(2,1)S(1)}, u32[]{:S(2)}, u32[]{:S(2)}) collective-permute-start(bf16[4,24,4096]{2,1,0:T(8,128)(2,1)S(1)} %pad_maximum_fusion.1.refs_0_), channel_id=1, source_target_pairs={{0,48},{1,49},{2,50},{3,51},{4,52},{5,53},{6,54},{7,55},{8,76},{9,... | collective-permute-start | bytes 2359304 | tf_op jit(solution)/shard_map/ppermute | solution.py:42
  32.9 25.2 %all-to-all-start.1 = ((bf16[16,24,1024]{2,1,0:T(8,128)(2,1)}), bf16[16,24,1024]{2,1,0:T(8,128)(2,1)}, u32[]{:S(2)}, u32[]{:S(2)}) async-start(bf16[16,24,1024]{2,1,0:T(8,128)(2,1)} %copy.37), calls=%async_computation.1 | async-start | bytes 1572864 | tf_op jit(solution)/shard_map/all_to_all | solution.py:120
  58.2 37.2 %collective-permute-start.10 = (bf16[384,4096]{1,0:T(8,128)(2,1)}, bf16[384,4096]{1,0:T(8,128)(2,1)}, u32[]{:S(2)}, u32[]{:S(2)}) collective-permute-start(bf16[384,4096]{1,0:T(8,128)(2,1)} %bitcast.97), channel_id=1, source_target_pairs={{0,8},{1,9},{2,10},{3,11},{4,12},{5,13},{6,14},{7,15},{8,0},{9,1},... | collective-permute-start | bytes 9437192 | tf_op jit(solution)/shard_map/ppermute | solution.py:30
  59.9 19.9 %collective-permute-start.9 = (bf16[2,4,2,24,1024]{4,3,2,1,0:T(8,128)(2,1)}, bf16[2,4,2,24,1024]{4,3,2,1,0:T(8,128)(2,1)S(1)}, u32[]{:S(2)}, u32[]{:S(2)}) collective-permute-start(bf16[2,4,2,24,1024]{4,3,2,1,0:T(8,128)(2,1)} %bitcast.12), channel_id=1, source_target_pairs={{0,4},{1,5},{2,6},{3,7},{4,0},{5,1},{6,2},{7,3},{8,12},{9,13},{10,... | collective-permute-start | bytes 2359304 | tf_op jit(solution)/shard_map/ppermute | solution.py:30
  81.9 53.6 %all-to-all-start.2 = ((bf16[16,4,24,1024]{3,2,1,0:T(8,128)(2,1)}), bf16[16,4,24,1024]{3,2,1,0:T(8,128)(2,1)}, u32[]{:S(2)}, u32[]{:S(2)}) async-start(bf16[16,4,24,1024]{3,2,1,0:T(8,128)(2,1)} %broadcast_in_dim.4), calls=%async_computation.2 | async-start | bytes 6291456 | tf_op jit(solution)/shard_map/all_to_all | solution.py:65
  89.1 187.7 %reduce-scatter.2.cloned.1.call-start = ((), (), s32[]{:S(2)}) async-start(), calls=%async_computation.7 | async-start | bytes 2621440 | tf_op jit(solution)/shard_map/reduce_scatter | solution.py:187
  95.3 18.1 %collective-permute-start.14 = (bf16[384,1024]{1,0:T(8,128)(2,1)S(1)}, bf16[384,1024]{1,0:T(8,128)(2,1)S(1)}, u32[]{:S(2)}, u32[]{:S(2)}) collective-permute-start(bf16[384,1024]{1,0:T(8,128)(2,1)S(1)} %multiply_convert_fusion.2), channel_id=1, source_target_pairs={{0,1},{1,0},{2,3},{3,2},{4,5},{5,4},{6,7},{7,6},{8,9},{9,8},{10,11... | collective-permute-start | bytes 2359304 | tf_op jit(solution)/shard_map/ppermute | solution.py:30
  95.5 18.9 %collective-permute-start.15 = (bf16[384,1024]{1,0:T(8,128)(2,1)S(1)}, bf16[384,1024]{1,0:T(8,128)(2,1)}, u32[]{:S(2)}, u32[]{:S(2)}) collective-permute-start(bf16[384,1024]{1,0:T(8,128)(2,1)S(1)} %multiply_convert_fusion.2), channel_id=1, source_target_pairs={{0,3},{1,2},{2,1},{3,0},{4,7},{5,6},{6,5},{7,4},{8,11},{9,10},{10,... | collective-permute-start | bytes 2359304 | tf_op jit(solution)/shard_map/ppermute | solution.py:30
  105.9 35.4 %collective-permute-start.11 = (bf16[384,1024]{1,0:T(8,128)(2,1)}, bf16[384,1024]{1,0:T(8,128)(2,1)}, u32[]{:S(2)}, u32[]{:S(2)}) collective-permute-start(bf16[384,1024]{1,0:T(8,128)(2,1)} %bitcast.19), channel_id=1, source_target_pairs={{0,4},{1,5},{2,6},{3,7},{4,0},{5,1},{6,2},{7,3},{8,12},{9,13},{10,... | collective-permute-start | bytes 2359304 | tf_op jit(solution)/shard_map/ppermute | solution.py:30
  109.4 32.0 %collective-permute-start.12 = (bf16[384,1024]{1,0:T(8,128)(2,1)}, bf16[384,1024]{1,0:T(8,128)(2,1)}, u32[]{:S(2)}, u32[]{:S(2)}) collective-permute-start(bf16[384,1024]{1,0:T(8,128)(2,1)} %multiply_convert_fusion), channel_id=1, source_target_pairs={{0,1},{1,0},{2,3},{3,2},{4,5},{5,4},{6,7},{7,6},{8,9},{9,8},{10,11... | collective-permute-start | bytes 2359304 | tf_op jit(solution)/shard_map/ppermute | solution.py:30
  110.0 31.3 %collective-permute-start.13 = (bf16[384,1024]{1,0:T(8,128)(2,1)}, bf16[384,1024]{1,0:T(8,128)(2,1)}, u32[]{:S(2)}, u32[]{:S(2)}) collective-permute-start(bf16[384,1024]{1,0:T(8,128)(2,1)} %multiply_convert_fusion), channel_id=1, source_target_pairs={{0,3},{1,2},{2,1},{3,0},{4,7},{5,6},{6,5},{7,4},{8,11},{9,10},{10,... | collective-permute-start | bytes 2359304 | tf_op jit(solution)/shard_map/ppermute | solution.py:30
  141.3 39.4 %collective-permute-start.16 = (bf16[384,4096]{1,0:T(8,128)(2,1)}, bf16[384,4096]{1,0:T(8,128)(2,1)}, u32[]{:S(2)}, u32[]{:S(2)}) collective-permute-start(bf16[384,4096]{1,0:T(8,128)(2,1)} %fusion.8), channel_id=1, source_target_pairs={{0,8},{1,9},{2,10},{3,11},{4,12},{5,13},{6,14},{7,15},{8,0},{9,1},... | collective-permute-start | bytes 9437192 | tf_op jit(solution)/shard_map/ppermute | solution.py:30
  151.5 62.7 %collective-permute-start.18 = (bf16[1536,1024]{1,0:T(8,128)(2,1)}, bf16[1536,1024]{1,0:T(8,128)(2,1)}, u32[]{:S(2)}, u32[]{:S(2)}) collective-permute-start(bf16[1536,1024]{1,0:T(8,128)(2,1)} %bitcast.31), channel_id=1, source_target_pairs={{0,8},{1,9},{2,10},{3,11},{4,12},{5,13},{6,14},{7,15},{8,0},{9,1},... | collective-permute-start | bytes 9437192 | tf_op jit(solution)/shard_map/ppermute | solution.py:30
  155.8 29.6 %all-to-all-start.3 = ((bf16[16,24,1024]{2,1,0:T(8,128)(2,1)}), bf16[16,24,1024]{2,1,0:T(8,128)(2,1)S(1)}, u32[]{:S(2)}, u32[]{:S(2)}) async-start(bf16[16,24,1024]{2,1,0:T(8,128)(2,1)} %bitcast.24), calls=%async_computation.3 | async-start | bytes 1572864 | tf_op jit(solution)/shard_map/all_to_all | solution.py:177
  169.3 29.7 %collective-permute-start.17 = (bf16[384,1024]{1,0:T(8,128)(2,1)}, bf16[384,1024]{1,0:T(8,128)(2,1)S(1)}, u32[]{:S(2)}, u32[]{:S(2)}) collective-permute-start(bf16[384,1024]{1,0:T(8,128)(2,1)} %collective-permute-done.15), channel_id=1, source_target_pairs={{0,1},{1,0},{2,3},{3,2},{4,5},{5,4},{6,7},{7,6},{8,9},{9,8},{10,11... | collective-permute-start | bytes 2359304 | tf_op jit(solution)/shard_map/ppermute | solution.py:30
  172.8 46.7 %collective-permute-start.19 = (bf16[384,1024]{1,0:T(8,128)(2,1)}, bf16[384,1024]{1,0:T(8,128)(2,1)}, u32[]{:S(2)}, u32[]{:S(2)}) collective-permute-start(bf16[384,1024]{1,0:T(8,128)(2,1)} %collective-permute-done.12), channel_id=1, source_target_pairs={{0,3},{1,2},{2,1},{3,0},{4,7},{5,6},{6,5},{7,4},{8,11},{9,10},{10,... | collective-permute-start | bytes 2359304 | tf_op jit(solution)/shard_map/ppermute | solution.py:30
  199.8 59.9 %all-to-all-start.4 = ((bf16[16,24,4096]{2,1,0:T(8,128)(2,1)}), bf16[16,24,4096]{2,1,0:T(8,128)(2,1)S(1)}, u32[]{:S(2)}, u32[]{:S(2)}) async-start(bf16[16,24,4096]{2,1,0:T(8,128)(2,1)} %bitcast.99), calls=%async_computation.4 | async-start | bytes 6291456 | tf_op jit(solution)/shard_map/all_to_all | solution.py:65
  224.0 43.8 %collective-permute-start.20 = (bf16[512,1024]{1,0:T(8,128)(2,1)}, bf16[512,1024]{1,0:T(8,128)(2,1)}, u32[]{:S(2)}, u32[]{:S(2)}) collective-permute-start(bf16[512,1024]{1,0:T(8,128)(2,1)} %get-tuple-element.60), channel_id=1, source_target_pairs={{0,4},{1,5},{2,6},{3,7},{4,0},{5,1},{6,2},{7,3},{8,12},{9,13},{10,... | collective-permute-start | bytes 3145736 | tf_op jit(solution)/shard_map/ppermute | solution.py:30
  261.2 14.1 %all-to-all-start.5 = ((bf16[16,8,24]{2,1,0:T(8,128)(2,1)}), bf16[16,8,24]{2,1,0:T(8,128)(2,1)}, u32[]{:S(2)}, u32[]{:S(2)}) async-start(bf16[16,8,24]{2,1,0:T(8,128)(2,1)} %copy.48), calls=%async_computation.5 | async-start | bytes 65536 | tf_op jit(solution)/shard_map/all_to_all | solution.py:198
  (22 other events, 178.2 us)
Sparse Core Ops, SparseCore 0:
  147.5 44.9 reduce-scatter.1

commit v2 on v0

--- a/solution.py
+++ b/solution.py
@@ -145,14 +145,14 @@
         return (d_hidden * slope).astype(BF)
 
     hidden_own, slope_own = forward(own)
-    hidden_own, back_z, t_y = lax.optimization_barrier((hidden_own, back_z, t_y))
-    wide = gather(t_y, PLANE)
+    hidden_own, back_z = lax.optimization_barrier((hidden_own, back_z))
     pair = jnp.where(zl == 0, jnp.stack([back, back_z]), jnp.stack([back_z, back]))
     pair = pair.transpose(3, 2, 0, 1, 4, 5)
     d_output = jnp.where(c == 0, pair, pair[::-1]).reshape(768, 1024)
 
     d_own = backward(d_output[:384], slope_own)
-    d_own, other = lax.optimization_barrier((d_own, other))
+    d_own, other, t_y = lax.optimization_barrier((d_own, other, t_y))
+    wide = gather(t_y, PLANE)
     near_own = (swap(d_own, y=1), swap(d_own, y=3))
     hidden_other, slope_other = forward(other)
     d_other = backward(d_output[384:], slope_other)
@@ -165,26 +165,32 @@
     d_late, near_own = lax.optimization_barrier((d_other, near_own))
     far_own = swap(near_own[1], y=1)
     dt_other = dot(d_late, half, ((1,), (1,))).astype(BF)
-    dt = dot(d_own, half, ((1,), (1,))) + swap(dt_other, c=1).astype(F32)
+
+    dt_far = swap(dt_other, c=1)
+    d_late, wide, near_other, theirs, dt_far = lax.optimization_barrier(
+        (d_own, wide, near_other, theirs, dt_far)
+    )
+    dt = dot(d_late, half, ((1,), (1,))) + dt_far.astype(F32)
     dt = dt.astype(BF)
-
-    dt, mine, near_other, wide = lax.optimization_barrier((dt, mine, near_other, wide))
+    d_trunk = lax.psum_scatter(
+        dt, AXES, axis_index_groups=PLANE, scatter_dimension=0, tiled=True
+    )
+
+    mine, hidden, _ = lax.optimization_barrier((mine, hidden, dt))
     far_other = swap(near_other[0], y=3)
     output = dot(mine, second_own, ((1,), (0,))) + dot(theirs, second_far, ((1,), (0,)))
     output = output.astype(BF).reshape(2, 4, 2, 24, 1024)
     output = jnp.where(c == 0, output, output[::-1])
     output = output.transpose(2, 1, 0, 3, 4).reshape(16, 24, 1024)
     outs = lax.all_to_all(output, "expert", 0, 0, tiled=True)
-    dt, outs, far_own = lax.optimization_barrier((dt, outs, far_own))
-    dt = exchange(dt.reshape(16, 24, 4096), PLANE)
-    d_trunk = jnp.sum(dt, axis=0, dtype=F32).astype(BF)
+    wide = after(wide, output)
     wide = wide.reshape(16, 4, 24, 1024).transpose(1, 0, 2, 3).reshape(1536, 1024)
     wide_other = swap(wide, c=1)
 
     ds = dot(hidden, d_output, ((0,), (0,))).astype(BF)
-    d_second = lax.psum_scatter(
-        ds, AXES, axis_index_groups=RING, scatter_dimension=0, tiled=True
-    )
+    ds, outs = lax.optimization_barrier((ds, outs))
+    ds = exchange(ds.reshape(4, 256, 1024), RING)
+    d_second = jnp.sum(ds, axis=0, dtype=F32).astype(BF)
 
     mixed = jnp.einsum(
         "etr,ero->rto", gate_rows, outs, preferred_element_type=F32
@@ -193,7 +199,7 @@
         "rto,ero->etr", d_mixed, outs, preferred_element_type=F32
     ).astype(BF)
 
-    d_gate = lax.all_to_all(after(d_gate, dt), "expert", 0, 0, tiled=True)
+    d_gate = lax.all_to_all(after(d_gate, ds), "expert", 0, 0, tiled=True)
     d_gate = d_gate.transpose(1, 0, 2).reshape(8, 384)
 
     tile = dot(wide[:1152], jnp.concatenate([d_own, *near_own]), ((0,), (0,)))

time: 305 us -> 300 us (0.984)
  the two profiles are of different devices: /device:TPU:49 before, /device:TPU:1 now
where the time goes in v2:
time: 300 us; the launch traced here: 299 us
  waiting for transfers between devices  98 us (33%)
  starting transfers between devices  70.4 us (23%)
  matrix products  67.4 us (22%)
  local copies, waits for them, and re-layouts  36.5 us (12%)
  between operations  14.4 us (5%)
  other arithmetic  11.4 us (4%)
    ppermute x15, waiting for transfers between devices, swap(): return lax.ppermute(v, AXES, pairs)  68.1 us
    dot_general x13, matrix products, dot(): return lax.dot_general(a, b, (dims, ((), ())), preferred_element_type=F32)  61.5 us
    ppermute x15, starting transfers between devices, swap(): return lax.ppermute(v, AXES, pairs)  18.8 us
    all_to_all x2, waiting for transfers between devices, exchange(): return lax.all_to_all(v, AXES, 0, 0, axis_index_groups=members, tiled=True)  14.8 us
    all_to_all x1, waiting for transfers between devices, on_device(): d_gate = lax.all_to_all(after(d_gate, ds), 'expert', 0, 0, tiled=True)  14.3 us
    all_to_all x2, starting transfers between devices, exchange(): return lax.all_to_all(v, AXES, 0, 0, axis_index_groups=members, tiled=True)  11.5 us
    ppermute x6, starting transfers between devices, swap_split(): return lax.ppermute(v, AXES, pairs)  10.1 us
    all_to_all x1, starting transfers between devices, on_device(): outs = lax.all_to_all(output, 'expert', 0, 0, tiled=True)  8.57 us
  transfers between devices with their start and end apart: 28, of which 11 were waited for; matrix products, arithmetic and copies ran while one was open for 32% of the time, Pallas kernels for 0%

profile of v2, /device:TPU:1, one launch (start us, length us, event | category | flops | bytes accessed | tf_op | source)
XLA Modules:
  0.0 298.8 jit_solution(13767954293326630764)
XLA Ops:
  7.2 3.7 %collective-permute-start.1 = (bf16[24,4096]{1,0:T(8,128)(2,1)}, bf16[24,4096]{1,0:T(8,128)(2,1)S(1)}, u32[]{:S(2)}, u32[]{:S(2)}) collective-permute-start(bf16[24,4096]{1,0:T(8,128)(2,1)} %param.5), channel_id=1, source_target_pairs={{0,4},{1,5},{2,6},{3,7},{4,0},{5,1},{6,2},{7,3},{8,40},{9,41},{10,... | collective-permute-start | bytes 589832 | tf_op jit(solution)/shard_map/ppermute | solution.py:42
  13.1 8.2 %all-to-all-start = ((bf16[16,8,24]{2,1,0:T(8,128)(2,1)}), bf16[16,8,24]{2,1,0:T(8,128)(2,1)}, u32[]{:S(2)}, u32[]{:S(2)}) async-start(bf16[16,8,24]{2,1,0:T(8,128)(2,1)} %copy.35), calls=%async_computation | async-start | bytes 65536 | tf_op jit(solution)/shard_map/all_to_all | solution.py:105
  22.4 4.3 %collective-permute-start.5 = (bf16[4,24,4096]{2,1,0:T(8,128)(2,1)S(1)}, bf16[4,24,4096]{2,1,0:T(8,128)(2,1)S(1)}, u32[]{:S(2)}, u32[]{:S(2)}) collective-permute-start(bf16[4,24,4096]{2,1,0:T(8,128)(2,1)S(1)} %pad_maximum_fusion.1.refs_0_), channel_id=1, source_target_pairs={{0,48},{1,49},{2,50},{3,51},{4,52},{5,53},{6,54},{7,55},{8,76},{9,... | collective-permute-start | bytes 2359304 | tf_op jit(solution)/shard_map/ppermute | solution.py:42
  32.7 5.1 %all-to-all-start.1 = ((bf16[16,24,1024]{2,1,0:T(8,128)(2,1)}), bf16[16,24,1024]{2,1,0:T(8,128)(2,1)}, u32[]{:S(2)}, u32[]{:S(2)}) async-start(bf16[16,24,1024]{2,1,0:T(8,128)(2,1)} %copy.37), calls=%async_computation.1 | async-start | bytes 1572864 | tf_op jit(solution)/shard_map/all_to_all | solution.py:120
  61.8 8.9 %multiply_convert_fusion.3 = (bf16[384,1024]{1,0:T(8,128)(2,1)}, f32[384,1024]{1,0:T(8,128)S(1)}) fusion(bf16[384,4096]{1,0:T(8,128)(2,1)} %bitcast.101, bf16[1,4096,2048]{2,1,0:T(8,128)(2,1)} %param.6, s32[]{:T(128)S(6)} %select_n.134), kind=kOutput, calls=%fused_computation.51 | convolution fusion | flops 3223191552 | bytes 13893636 | tf_op jit(solution)/shard_map/dot_general | solution.py:69
  70.8 9.2 %collective-permute-done.9 = bf16[2,4,2,24,1024]{4,3,2,1,0:T(8,128)(2,1)S(1)} collective-permute-done((bf16[2,4,2,24,1024]{4,3,2,1,0:T(8,128)(2,1)}, bf16[2,4,2,24,1024]{4,3,2,1,0:T(8,128)(2,1)S(1)}, u32[]{:S(2)}, u32[]{:S(2)}) %collective-permute-start.9) | collective-permute-done | bytes 786464 | tf_op jit(solution)/shard_map/ppermute | solution.py:30
  87.6 6.4 %multiply_convert_fusion.1 = (bf16[384,1024]{1,0:T(8,128)(2,1)}, f32[384,1024]{1,0:T(8,128)S(1)}) fusion(bf16[384,4096]{1,0:T(8,128)(2,1)} %collective-permute-done.10, bf16[1,4096,2048]{2,1,0:T(8,128)(2,1)S(1)} %bitcast.124, s32[]{:T(128)S(6)} %select_n.134), kind=kOutput, calls=%fused_computation.48 | convolution fusion | flops 3223191552 | bytes 13893636 | tf_op jit(solution)/shard_map/dot_general | solution.py:69
  96.2 9.3 %collective-permute-done.15 = bf16[384,1024]{1,0:T(8,128)(2,1)} collective-permute-done((bf16[384,1024]{1,0:T(8,128)(2,1)S(1)}, bf16[384,1024]{1,0:T(8,128)(2,1)}, u32[]{:S(2)}, u32[]{:S(2)}) %collective-permute-start.15) | collective-permute-done | bytes 786464 | tf_op jit(solution)/shard_map/ppermute | solution.py:30
  105.9 6.0 %fusion.10 = bf16[384,4096]{1,0:T(8,128)(2,1)} fusion(bf16[384,1024]{1,0:T(8,128)(2,1)} %multiply_convert_fusion, bf16[1,4096,2048]{2,1,0:T(8,128)(2,1)S(1)} %bitcast.124, s32[]{:T(128)S(6)} %select_n.134), kind=kOutput, calls=%fused_computation.9 | convolution fusion | flops 3222798336 | bytes 12320772 | tf_op jit(solution)/shard_map/dot_general | solution.py:69
  115.8 7.6 %all-to-all-start.2 = ((bf16[16,4,24,1024]{3,2,1,0:T(8,128)(2,1)}), bf16[16,4,24,1024]{3,2,1,0:T(8,128)(2,1)}, u32[]{:S(2)}, u32[]{:S(2)}) async-start(bf16[16,4,24,1024]{3,2,1,0:T(8,128)(2,1)} %broadcast_in_dim.4), calls=%async_computation.2 | async-start | bytes 6291456 | tf_op jit(solution)/shard_map/all_to_all | solution.py:65
  128.9 15.0 %collective-permute-done.12 = bf16[384,1024]{1,0:T(8,128)(2,1)} collective-permute-done((bf16[384,1024]{1,0:T(8,128)(2,1)}, bf16[384,1024]{1,0:T(8,128)(2,1)}, u32[]{:S(2)}, u32[]{:S(2)}) %collective-permute-start.12) | collective-permute-done | bytes 786464 | tf_op jit(solution)/shard_map/ppermute | solution.py:30
  143.9 32.2 %collective-permute-done.13 = bf16[384,1024]{1,0:T(8,128)(2,1)} collective-permute-done((bf16[384,1024]{1,0:T(8,128)(2,1)}, bf16[384,1024]{1,0:T(8,128)(2,1)}, u32[]{:S(2)}, u32[]{:S(2)}) %collective-permute-start.13) | collective-permute-done | bytes 786464 | tf_op jit(solution)/shard_map/ppermute | solution.py:30
  176.1 4.1 %all-to-all-done.2 = bf16[16,4,24,1024]{3,2,1,0:T(8,128)(2,1)} async-done(((bf16[16,4,24,1024]{3,2,1,0:T(8,128)(2,1)}), bf16[16,4,24,1024]{3,2,1,0:T(8,128)(2,1)}, u32[]{:S(2)}, u32[]{:S(2)}) %all-to-all-start.2) | async-done | bytes 3145760 | tf_op jit(solution)/shard_map/all_to_all | solution.py:65
  180.2 9.6 %add_convert_fusion = bf16[384,4096]{1,0:T(8,128)(2,1)} fusion(bf16[384,4096]{1,0:T(8,128)(2,1)} %collective-permute-done.16, bf16[384,1024]{1,0:T(8,128)(2,1)} %copy-done.9, bf16[1,4096,2048]{2,1,0:T(8,128)(2,1)} %param.6, s32[]{:T(128)S(6)} %select_n.134), kind=kOutput, calls=%fused_computation.8 | convolution fusion | flops 3225944064 | bytes 15466500 | tf_op jit(solution)/shard_map/dot_general | solution.py:69
  196.2 3.9 %copy.65 = bf16[16,4,24,1024]{3,2,0,1:T(8,128)(2,1)} copy(bf16[16,4,24,1024]{3,2,1,0:T(8,128)(2,1)} %all-to-all-done.2) | data formatting | bytes 6291456 | tf_op jit(solution)/shard_map/optimization_barrier | solution.py:46
  203.0 8.6 %all-to-all-start.3 = ((bf16[16,24,1024]{2,1,0:T(8,128)(2,1)}), bf16[16,24,1024]{2,1,0:T(8,128)(2,1)S(1)}, u32[]{:S(2)}, u32[]{:S(2)}) async-start(bf16[16,24,1024]{2,1,0:T(8,128)(2,1)} %bitcast.105), calls=%async_computation.3 | async-start | bytes 1572864 | tf_op jit(solution)/shard_map/all_to_all | solution.py:185
  215.9 6.0 %fusion.19 = f32[1024,1024]{1,0:T(8,128)} fusion(bf16[1152,1024]{1,0:T(8,128)(2,1)S(1)} %bitcast.106, bf16[384,1024]{1,0:T(8,128)(2,1)} %collective-permute-done.15, bf16[384,1024]{1,0:T(8,128)(2,1)} %collective-permute-done.14, bf16[384,1024]{1,0:T(8,128)(2,1)S(1)} %copy-done.10), kind=kOutput, calls=%fused_computation.18 | convolution fusion | flops 2422996992 | bytes 8912896 | tf_op jit(solution)/shard_map/dot_general | solution.py:69
  225.1 4.5 %fusion.71 = f32[1024,1024]{1,0:T(8,128)} fusion(bf16[384,1024]{1,0:T(8,128)(2,1)S(1)} %bitcast.104, bf16[384,1024]{1,0:T(8,128)(2,1)} %collective-permute-done.18), kind=kOutput, calls=%fused_computation.94 | convolution fusion | flops 805306368 | bytes 5767168 | tf_op jit(solution)/shard_map/dot_general | solution.py:69
  229.5 3.9 %all-to-all-start.4 = ((bf16[4,256,1024]{2,1,0:T(8,128)(2,1)}), bf16[4,256,1024]{2,1,0:T(8,128)(2,1)S(1)}, u32[]{:S(2)}, u32[]{:S(2)}) async-start(bf16[4,256,1024]{2,1,0:T(8,128)(2,1)} %bitcast.107), calls=%async_computation.5 | async-start | bytes 4194304 | tf_op jit(solution)/shard_map/all_to_all | solution.py:65
  233.4 5.4 %fusion.17 = f32[1024,1024]{1,0:T(8,128)S(1)} fusion(bf16[1536,1024]{1,0:T(8,128)(2,1)} %collective-permute-done.17, bf16[384,1024]{1,0:T(8,128)(2,1)} %collective-permute-done.12, bf16[384,1024]{1,0:T(8,128)(2,1)} %collective-permute-done.11, bf16[384,1024]{1,0:T(8,128)(2,1)} %multiply_convert_fusion), kind=kOutput, calls=%fused_computation.16 | convolution fusion | flops 2422996992 | bytes 8912896 | tf_op jit(solution)/shard_map/dot_general | solution.py:69
  248.5 10.7 %all-to-all-done.4 = bf16[4,256,1024]{2,1,0:T(8,128)(2,1)S(1)} async-done(((bf16[4,256,1024]{2,1,0:T(8,128)(2,1)}), bf16[4,256,1024]{2,1,0:T(8,128)(2,1)S(1)}, u32[]{:S(2)}, u32[]{:S(2)}) %all-to-all-start.4) | async-done | bytes 2097184 | tf_op jit(solution)/shard_map/all_to_all | solution.py:65
  260.7 8.1 %all-to-all-start.5 = ((bf16[16,8,24]{2,1,0:T(8,128)(2,1)}), bf16[16,8,24]{2,1,0:T(8,128)(2,1)}, u32[]{:S(2)}, u32[]{:S(2)}) async-start(bf16[16,8,24]{2,1,0:T(8,128)(2,1)} %copy.49), calls=%async_computation.6 | async-start | bytes 65536 | tf_op jit(solution)/shard_map/all_to_all | solution.py:202
  272.5 14.3 %all-to-all-done.5 = bf16[16,8,24]{2,1,0:T(8,128)(2,1)} async-done(((bf16[16,8,24]{2,1,0:T(8,128)(2,1)}), bf16[16,8,24]{2,1,0:T(8,128)(2,1)}, u32[]{:S(2)}, u32[]{:S(2)}) %all-to-all-start.5) | async-done | bytes 6176 | tf_op jit(solution)/shard_map/all_to_all | solution.py:202
  288.3 3.7 %maximum_select_fusion = bf16[1,512,2048]{2,1,0:T(8,128)(2,1)} fusion(bf16[1,512,1024]{2,1,0:T(8,128)(2,1)} %bitcast.36, bf16[1,512,1024]{2,1,0:T(8,128)(2,1)S(1)} %get-tuple-element.61, pred[]{:T(512)S(6)} %eq.17), kind=kLoop, calls=%fused_computation.29 | loop fusion | flops 9437184 | bytes 4194305 | tf_op jit(solution)/shard_map/jit(_where)/select_n | solution.py:212
  (115 shorter events, 85.8 us)
Async XLA Ops:
  7.2 14.1 %collective-permute-start.1 = (bf16[24,4096]{1,0:T(8,128)(2,1)}, bf16[24,4096]{1,0:T(8,128)(2,1)S(1)}, u32[]{:S(2)}, u32[]{:S(2)}) collective-permute-start(bf16[24,4096]{1,0:T(8,128)(2,1)} %param.5), channel_id=1, source_target_pairs={{0,4},{1,5},{2,6},{3,7},{4,0},{5,1},{6,2},{7,3},{8,40},{9,41},{10,... | collective-permute-start | bytes 589832 | tf_op jit(solution)/shard_map/ppermute | solution.py:42
  10.8 10.5 %collective-permute-start = (bf16[24,4096]{1,0:T(8,128)(2,1)}, bf16[24,4096]{1,0:T(8,128)(2,1)S(1)}, u32[]{:S(2)}, u32[]{:S(2)}) collective-permute-start(bf16[24,4096]{1,0:T(8,128)(2,1)} %param.5), channel_id=1, source_target_pairs={{0,64},{1,65},{2,66},{3,67},{4,68},{5,69},{6,70},{7,71},{8,24},{9,... | collective-permute-start | bytes 589832 | tf_op jit(solution)/shard_map/ppermute | solution.py:42
  13.1 15.6 %all-to-all-start = ((bf16[16,8,24]{2,1,0:T(8,128)(2,1)}), bf16[16,8,24]{2,1,0:T(8,128)(2,1)}, u32[]{:S(2)}, u32[]{:S(2)}) async-start(bf16[16,8,24]{2,1,0:T(8,128)(2,1)} %copy.35), calls=%async_computation | async-start | bytes 65536 | tf_op jit(solution)/shard_map/all_to_all | solution.py:105
  22.4 33.5 %collective-permute-start.5 = (bf16[4,24,4096]{2,1,0:T(8,128)(2,1)S(1)}, bf16[4,24,4096]{2,1,0:T(8,128)(2,1)S(1)}, u32[]{:S(2)}, u32[]{:S(2)}) collective-permute-start(bf16[4,24,4096]{2,1,0:T(8,128)(2,1)S(1)} %pad_maximum_fusion.1.refs_0_), channel_id=1, source_target_pairs={{0,48},{1,49},{2,50},{3,51},{4,52},{5,53},{6,54},{7,55},{8,76},{9,... | collective-permute-start | bytes 2359304 | tf_op jit(solution)/shard_map/ppermute | solution.py:42
  26.7 29.1 %collective-permute-start.4 = (bf16[4,24,4096]{2,1,0:T(8,128)(2,1)S(1)}, bf16[4,24,4096]{2,1,0:T(8,128)(2,1)S(1)}, u32[]{:S(2)}, u32[]{:S(2)}) collective-permute-start(bf16[4,24,4096]{2,1,0:T(8,128)(2,1)S(1)} %pad_maximum_fusion.1.refs_0_), channel_id=1, source_target_pairs={{0,32},{1,33},{2,34},{3,35},{4,36},{5,37},{6,38},{7,39},{8,12},{9,... | collective-permute-start | bytes 2359304 | tf_op jit(solution)/shard_map/ppermute | solution.py:42
  26.7 29.1 %collective-permute-start.3 = (bf16[4,24,4096]{2,1,0:T(8,128)(2,1)S(1)}, bf16[4,24,4096]{2,1,0:T(8,128)(2,1)S(1)}, u32[]{:S(2)}, u32[]{:S(2)}) collective-permute-start(bf16[4,24,4096]{2,1,0:T(8,128)(2,1)S(1)} %pad_maximum_fusion.1.refs_0_), channel_id=1, source_target_pairs={{0,16},{1,17},{2,18},{3,19},{4,20},{5,21},{6,22},{7,23},{8,72},{9,... | collective-permute-start | bytes 2359304 | tf_op jit(solution)/shard_map/ppermute | solution.py:42
  32.7 25.6 %all-to-all-start.1 = ((bf16[16,24,1024]{2,1,0:T(8,128)(2,1)}), bf16[16,24,1024]{2,1,0:T(8,128)(2,1)}, u32[]{:S(2)}, u32[]{:S(2)}) async-start(bf16[16,24,1024]{2,1,0:T(8,128)(2,1)} %copy.37), calls=%async_computation.1 | async-start | bytes 1572864 | tf_op jit(solution)/shard_map/all_to_all | solution.py:120
  58.3 27.3 %collective-permute-start.10 = (bf16[384,4096]{1,0:T(8,128)(2,1)}, bf16[384,4096]{1,0:T(8,128)(2,1)}, u32[]{:S(2)}, u32[]{:S(2)}) collective-permute-start(bf16[384,4096]{1,0:T(8,128)(2,1)} %bitcast.100), channel_id=1, source_target_pairs={{0,8},{1,9},{2,10},{3,11},{4,12},{5,13},{6,14},{7,15},{8,0},{9,1},... | collective-permute-start | bytes 9437192 | tf_op jit(solution)/shard_map/ppermute | solution.py:30
  59.9 20.0 %collective-permute-start.9 = (bf16[2,4,2,24,1024]{4,3,2,1,0:T(8,128)(2,1)}, bf16[2,4,2,24,1024]{4,3,2,1,0:T(8,128)(2,1)S(1)}, u32[]{:S(2)}, u32[]{:S(2)}) collective-permute-start(bf16[2,4,2,24,1024]{4,3,2,1,0:T(8,128)(2,1)} %bitcast.11), channel_id=1, source_target_pairs={{0,4},{1,5},{2,6},{3,7},{4,0},{5,1},{6,2},{7,3},{8,12},{9,13},{10,... | collective-permute-start | bytes 2359304 | tf_op jit(solution)/shard_map/ppermute | solution.py:30
  85.6 19.9 %collective-permute-start.15 = (bf16[384,1024]{1,0:T(8,128)(2,1)S(1)}, bf16[384,1024]{1,0:T(8,128)(2,1)}, u32[]{:S(2)}, u32[]{:S(2)}) collective-permute-start(bf16[384,1024]{1,0:T(8,128)(2,1)S(1)} %multiply_convert_fusion.2), channel_id=1, source_target_pairs={{0,3},{1,2},{2,1},{3,0},{4,7},{5,6},{6,5},{7,4},{8,11},{9,10},{10,... | collective-permute-start | bytes 2359304 | tf_op jit(solution)/shard_map/ppermute | solution.py:30
  87.6 18.3 %collective-permute-start.14 = (bf16[384,1024]{1,0:T(8,128)(2,1)S(1)}, bf16[384,1024]{1,0:T(8,128)(2,1)}, u32[]{:S(2)}, u32[]{:S(2)}) collective-permute-start(bf16[384,1024]{1,0:T(8,128)(2,1)S(1)} %multiply_convert_fusion.2), channel_id=1, source_target_pairs={{0,1},{1,0},{2,3},{3,2},{4,5},{5,4},{6,7},{7,6},{8,9},{9,8},{10,11... | collective-permute-start | bytes 2359304 | tf_op jit(solution)/shard_map/ppermute | solution.py:30
  111.9 68.3 %collective-permute-start.16 = (bf16[384,4096]{1,0:T(8,128)(2,1)}, bf16[384,4096]{1,0:T(8,128)(2,1)}, u32[]{:S(2)}, u32[]{:S(2)}) collective-permute-start(bf16[384,4096]{1,0:T(8,128)(2,1)} %fusion.10), channel_id=1, source_target_pairs={{0,8},{1,9},{2,10},{3,11},{4,12},{5,13},{6,14},{7,15},{8,0},{9,1},... | collective-permute-start | bytes 9437192 | tf_op jit(solution)/shard_map/ppermute | solution.py:30
  115.8 64.5 %all-to-all-start.2 = ((bf16[16,4,24,1024]{3,2,1,0:T(8,128)(2,1)}), bf16[16,4,24,1024]{3,2,1,0:T(8,128)(2,1)}, u32[]{:S(2)}, u32[]{:S(2)}) async-start(bf16[16,4,24,1024]{3,2,1,0:T(8,128)(2,1)} %broadcast_in_dim.4), calls=%async_computation.2 | async-start | bytes 6291456 | tf_op jit(solution)/shard_map/all_to_all | solution.py:65
  123.4 168.6 %reduce-scatter.2.cloned.1.call-start = ((), (), s32[]{:S(2)}) async-start(), calls=%async_computation.7 | async-start | bytes 3342336 | tf_op jit(solution)/shard_map/reduce_scatter | solution.py:175
  123.4 20.5 %collective-permute-start.12 = (bf16[384,1024]{1,0:T(8,128)(2,1)}, bf16[384,1024]{1,0:T(8,128)(2,1)}, u32[]{:S(2)}, u32[]{:S(2)}) collective-permute-start(bf16[384,1024]{1,0:T(8,128)(2,1)} %multiply_convert_fusion), channel_id=1, source_target_pairs={{0,3},{1,2},{2,1},{3,0},{4,7},{5,6},{6,5},{7,4},{8,11},{9,10},{10,... | collective-permute-start | bytes 2359304 | tf_op jit(solution)/shard_map/ppermute | solution.py:30
  124.7 19.2 %collective-permute-start.11 = (bf16[384,1024]{1,0:T(8,128)(2,1)}, bf16[384,1024]{1,0:T(8,128)(2,1)}, u32[]{:S(2)}, u32[]{:S(2)}) collective-permute-start(bf16[384,1024]{1,0:T(8,128)(2,1)} %multiply_convert_fusion), channel_id=1, source_target_pairs={{0,1},{1,0},{2,3},{3,2},{4,5},{5,4},{6,7},{7,6},{8,9},{9,8},{10,11... | collective-permute-start | bytes 2359304 | tf_op jit(solution)/shard_map/ppermute | solution.py:30
  127.6 48.5 %collective-permute-start.13 = (bf16[384,1024]{1,0:T(8,128)(2,1)}, bf16[384,1024]{1,0:T(8,128)(2,1)}, u32[]{:S(2)}, u32[]{:S(2)}) collective-permute-start(bf16[384,1024]{1,0:T(8,128)(2,1)} %bitcast.20), channel_id=1, source_target_pairs={{0,4},{1,5},{2,6},{3,7},{4,0},{5,1},{6,2},{7,3},{8,12},{9,13},{10,... | collective-permute-start | bytes 2359304 | tf_op jit(solution)/shard_map/ppermute | solution.py:30
  200.1 33.3 %collective-permute-start.17 = (bf16[1536,1024]{1,0:T(8,128)(2,1)}, bf16[1536,1024]{1,0:T(8,128)(2,1)}, u32[]{:S(2)}, u32[]{:S(2)}) collective-permute-start(bf16[1536,1024]{1,0:T(8,128)(2,1)} %bitcast.32), channel_id=1, source_target_pairs={{0,8},{1,9},{2,10},{3,11},{4,12},{5,13},{6,14},{7,15},{8,0},{9,1},... | collective-permute-start | bytes 9437192 | tf_op jit(solution)/shard_map/ppermute | solution.py:30
  203.0 22.1 %collective-permute-start.18 = (bf16[384,1024]{1,0:T(8,128)(2,1)}, bf16[384,1024]{1,0:T(8,128)(2,1)}, u32[]{:S(2)}, u32[]{:S(2)}) collective-permute-start(bf16[384,1024]{1,0:T(8,128)(2,1)} %collective-permute-done.15), channel_id=1, source_target_pairs={{0,1},{1,0},{2,3},{3,2},{4,5},{5,4},{6,7},{7,6},{8,9},{9,8},{10,11... | collective-permute-start | bytes 2359304 | tf_op jit(solution)/shard_map/ppermute | solution.py:30
  203.0 26.5 %all-to-all-start.3 = ((bf16[16,24,1024]{2,1,0:T(8,128)(2,1)}), bf16[16,24,1024]{2,1,0:T(8,128)(2,1)S(1)}, u32[]{:S(2)}, u32[]{:S(2)}) async-start(bf16[16,24,1024]{2,1,0:T(8,128)(2,1)} %bitcast.105), calls=%async_computation.3 | async-start | bytes 1572864 | tf_op jit(solution)/shard_map/all_to_all | solution.py:185
  214.8 24.1 %collective-permute-start.19 = (bf16[384,1024]{1,0:T(8,128)(2,1)}, bf16[384,1024]{1,0:T(8,128)(2,1)}, u32[]{:S(2)}, u32[]{:S(2)}) collective-permute-start(bf16[384,1024]{1,0:T(8,128)(2,1)} %collective-permute-done.11), channel_id=1, source_target_pairs={{0,3},{1,2},{2,1},{3,0},{4,7},{5,6},{6,5},{7,4},{8,11},{9,10},{10,... | collective-permute-start | bytes 2359304 | tf_op jit(solution)/shard_map/ppermute | solution.py:30
  229.5 29.6 %all-to-all-start.4 = ((bf16[4,256,1024]{2,1,0:T(8,128)(2,1)}), bf16[4,256,1024]{2,1,0:T(8,128)(2,1)S(1)}, u32[]{:S(2)}, u32[]{:S(2)}) async-start(bf16[4,256,1024]{2,1,0:T(8,128)(2,1)} %bitcast.107), calls=%async_computation.5 | async-start | bytes 4194304 | tf_op jit(solution)/shard_map/all_to_all | solution.py:65
  243.1 45.2 %collective-permute-start.20 = (bf16[512,1024]{1,0:T(8,128)(2,1)}, bf16[512,1024]{1,0:T(8,128)(2,1)}, u32[]{:S(2)}, u32[]{:S(2)}) collective-permute-start(bf16[512,1024]{1,0:T(8,128)(2,1)} %get-tuple-element.62), channel_id=1, source_target_pairs={{0,4},{1,5},{2,6},{3,7},{4,0},{5,1},{6,2},{7,3},{8,12},{9,13},{10,... | collective-permute-start | bytes 3145736 | tf_op jit(solution)/shard_map/ppermute | solution.py:30
  260.7 26.1 %all-to-all-start.5 = ((bf16[16,8,24]{2,1,0:T(8,128)(2,1)}), bf16[16,8,24]{2,1,0:T(8,128)(2,1)}, u32[]{:S(2)}, u32[]{:S(2)}) async-start(bf16[16,8,24]{2,1,0:T(8,128)(2,1)} %copy.49), calls=%async_computation.6 | async-start | bytes 65536 | tf_op jit(solution)/shard_map/all_to_all | solution.py:202
  (19 other events, 192.5 us)
Sparse Core Ops, SparseCore 0:
  190.0 88.2 reduce-scatter.1

commit v3 on v1

--- a/solution.py
+++ b/solution.py
@@ -145,14 +145,14 @@
         return (d_hidden * slope).astype(BF)
 
     hidden_own, slope_own = forward(own)
-    hidden_own, back_z, t_y = lax.optimization_barrier((hidden_own, back_z, t_y))
-    wide = gather(t_y, PLANE)
+    hidden_own, back_z = lax.optimization_barrier((hidden_own, back_z))
     pair = jnp.where(zl == 0, jnp.stack([back, back_z]), jnp.stack([back_z, back]))
     pair = pair.transpose(3, 2, 0, 1, 4, 5)
     d_output = jnp.where(c == 0, pair, pair[::-1]).reshape(768, 1024)
 
     d_own = backward(d_output[:384], slope_own)
-    d_own, other = lax.optimization_barrier((d_own, other))
+    d_own, other, t_y = lax.optimization_barrier((d_own, other, t_y))
+    wide = gather(t_y, PLANE)
     near_own = (swap(d_own, y=1), swap(d_own, y=3))
     hidden_other, slope_other = forward(other)
     d_other = backward(d_output[384:], slope_other)
@@ -166,18 +166,20 @@
     far_own = swap(near_own[1], y=1)
     dt_other = dot(d_late, half, ((1,), (1,))).astype(BF)
 
-    mine, theirs, near_other, wide, dt_other = lax.optimization_barrier(
-        (mine, theirs, near_other, wide, dt_other)
-    )
+    d_late, wide, near_other, dt_other, theirs = lax.optimization_barrier(
+        (d_own, wide, near_other, dt_other, theirs)
+    )
+    dt_far = swap(dt_other, c=1)
     far_other = swap(near_other[0], y=3)
+
     output = dot(mine, second_own, ((1,), (0,))) + dot(theirs, second_far, ((1,), (0,)))
     output = output.astype(BF).reshape(2, 4, 2, 24, 1024)
     output = jnp.where(c == 0, output, output[::-1])
     output = output.transpose(2, 1, 0, 3, 4).reshape(16, 24, 1024)
     outs = lax.all_to_all(output, "expert", 0, 0, tiled=True)
-    dt = dot(after(d_own, output), half, ((1,), (1,))) + swap(dt_other, c=1).astype(F32)
-    dt = dt.astype(BF)
-    dt, outs, far_own = lax.optimization_barrier((dt, outs, far_own))
+    d_late, hidden, wide, _ = lax.optimization_barrier((d_late, hidden, wide, output))
+    dt = dot(d_late, half, ((1,), (1,))) + dt_far.astype(F32)
+    dt, outs = lax.optimization_barrier((dt.astype(BF), outs))
     dt = exchange(dt.reshape(16, 24, 4096), PLANE)
     d_trunk = jnp.sum(dt, axis=0, dtype=F32).astype(BF)
     wide = wide.reshape(16, 4, 24, 1024).transpose(1, 0, 2, 3).reshape(1536, 1024)

time: 288 us -> 285 us (0.990)
  waiting for transfers between devices: 79.9 us -> 70 us
  matrix products: 58.5 us -> 65.4 us
    all_to_all x2, waiting for transfers between devices: 43 us -> 29.9 us  [exchange(): return lax.all_to_all(v, AXES, 0, 0, axis_index_groups=members, tiled=True)]
    dot_general x13, matrix products: 52.6 us -> 59.4 us  [dot(): return lax.dot_general(a, b, (dims, ((), ())), preferred_element_type=F32)]
    ppermute x15, waiting for transfers between devices: 33.3 us -> 37.5 us  [swap(): return lax.ppermute(v, AXES, pairs)]
    unnamed x39 -> x31, local copies, waits for them, and re-layouts: 10.5 us -> 8.56 us
  transfers between devices with their start and end apart: 28 -> 28, of which waited for: 12 -> 11; matrix products, arithmetic and copies ran while one was open for 38% -> 40% of each run, Pallas kernels for 0% -> 0%
where the time goes in v3:
time: 285 us; the launch traced here: 282 us
  starting transfers between devices  76.8 us (27%)
  waiting for transfers between devices  70 us (25%)
  matrix products  65.4 us (23%)
  local copies, waits for them, and re-layouts  39.4 us (14%)
  other arithmetic  15.4 us (5%)
  between operations  14.4 us (5%)
    dot_general x13, matrix products, dot(): return lax.dot_general(a, b, (dims, ((), ())), preferred_element_type=F32)  59.4 us
    ppermute x15, waiting for transfers between devices, swap(): return lax.ppermute(v, AXES, pairs)  37.5 us
    all_to_all x2, waiting for transfers between devices, exchange(): return lax.all_to_all(v, AXES, 0, 0, axis_index_groups=members, tiled=True)  29.9 us
    ppermute x15, starting transfers between devices, swap(): return lax.ppermute(v, AXES, pairs)  19.1 us
    all_to_all x2, starting transfers between devices, exchange(): return lax.all_to_all(v, AXES, 0, 0, axis_index_groups=members, tiled=True)  15.6 us
    all_to_all x1, starting transfers between devices, on_device(): outs = lax.all_to_all(output, 'expert', 0, 0, tiled=True)  13.1 us
    ppermute x6, starting transfers between devices, swap_split(): return lax.ppermute(v, AXES, pairs)  10.1 us
    unnamed x31, local copies, waits for them, and re-layouts  8.56 us
  transfers between devices with their start and end apart: 28, of which 11 were waited for; matrix products, arithmetic and copies ran while one was open for 40% of the time, Pallas kernels for 0%

profile of v3, /device:TPU:1, one launch (start us, length us, event | category | flops | bytes accessed | tf_op | source)
XLA Modules:
  0.0 282.1 jit_solution(4345448640958111761)
XLA Ops:
  7.2 3.7 %collective-permute-start.1 = (bf16[24,4096]{1,0:T(8,128)(2,1)}, bf16[24,4096]{1,0:T(8,128)(2,1)S(1)}, u32[]{:S(2)}, u32[]{:S(2)}) collective-permute-start(bf16[24,4096]{1,0:T(8,128)(2,1)} %param.5), channel_id=1, source_target_pairs={{0,4},{1,5},{2,6},{3,7},{4,0},{5,1},{6,2},{7,3},{8,40},{9,41},{10,... | collective-permute-start | bytes 589832 | tf_op jit(solution)/shard_map/ppermute | solution.py:42
  13.1 8.2 %all-to-all-start = ((bf16[16,8,24]{2,1,0:T(8,128)(2,1)}), bf16[16,8,24]{2,1,0:T(8,128)(2,1)}, u32[]{:S(2)}, u32[]{:S(2)}) async-start(bf16[16,8,24]{2,1,0:T(8,128)(2,1)} %copy.35), calls=%async_computation | async-start | bytes 65536 | tf_op jit(solution)/shard_map/all_to_all | solution.py:105
  22.4 4.3 %collective-permute-start.5 = (bf16[4,24,4096]{2,1,0:T(8,128)(2,1)S(1)}, bf16[4,24,4096]{2,1,0:T(8,128)(2,1)S(1)}, u32[]{:S(2)}, u32[]{:S(2)}) collective-permute-start(bf16[4,24,4096]{2,1,0:T(8,128)(2,1)S(1)} %pad_maximum_fusion.1.refs_0_), channel_id=1, source_target_pairs={{0,48},{1,49},{2,50},{3,51},{4,52},{5,53},{6,54},{7,55},{8,76},{9,... | collective-permute-start | bytes 2359304 | tf_op jit(solution)/shard_map/ppermute | solution.py:42
  32.7 5.1 %all-to-all-start.1 = ((bf16[16,24,1024]{2,1,0:T(8,128)(2,1)}), bf16[16,24,1024]{2,1,0:T(8,128)(2,1)}, u32[]{:S(2)}, u32[]{:S(2)}) async-start(bf16[16,24,1024]{2,1,0:T(8,128)(2,1)} %copy.37), calls=%async_computation.1 | async-start | bytes 1572864 | tf_op jit(solution)/shard_map/all_to_all | solution.py:120
  39.5 3.2 %dynamic-slice_reduce_fusion.3 = (bf16[24,2,512]{2,1,0:T(2,128)(2,1)}, bf16[24,2,512]{2,1,0:T(2,128)(2,1)}, bf16[24,2,512]{2,1,0:T(2,128)(2,1)}, bf16[24,2,512]{2,1,0:T(2,128)(2,1)S(1)}) fusion(bf16[24,2,4,512]{3,2,1,0:T(4,128)(2,1)} %reshape.121, s32[]{:T(128)S(6)} %select_n.132, s32[]{:T(128)S(6)} %select_n.134, s32[]{:T(128)S(6)} %select_n.133, ...), kind=kLoop, calls=%fused_computation.71 | loop fusion | bytes 393232 | tf_op jit(solution)/shard_map/jit(dynamic_index_in_dim)/dynamic_slice | solution.py:73
  61.8 8.8 %multiply_convert_fusion.3 = (bf16[384,1024]{1,0:T(8,128)(2,1)}, f32[384,1024]{1,0:T(8,128)S(1)}) fusion(bf16[384,4096]{1,0:T(8,128)(2,1)} %bitcast.99, bf16[1,4096,2048]{2,1,0:T(8,128)(2,1)} %param.6, s32[]{:T(128)S(6)} %select_n.136), kind=kOutput, calls=%fused_computation.51 | convolution fusion | flops 3223191552 | bytes 13893636 | tf_op jit(solution)/shard_map/dot_general | solution.py:69
  70.5 9.3 %collective-permute-done.9 = bf16[2,4,2,24,1024]{4,3,2,1,0:T(8,128)(2,1)S(1)} collective-permute-done((bf16[2,4,2,24,1024]{4,3,2,1,0:T(8,128)(2,1)}, bf16[2,4,2,24,1024]{4,3,2,1,0:T(8,128)(2,1)S(1)}, u32[]{:S(2)}, u32[]{:S(2)}) %collective-permute-start.9) | collective-permute-done | bytes 786464 | tf_op jit(solution)/shard_map/ppermute | solution.py:30
  88.4 7.6 %all-to-all-start.2 = ((bf16[16,4,24,1024]{3,2,1,0:T(8,128)(2,1)}), bf16[16,4,24,1024]{3,2,1,0:T(8,128)(2,1)}, u32[]{:S(2)}, u32[]{:S(2)}) async-start(bf16[16,4,24,1024]{3,2,1,0:T(8,128)(2,1)} %broadcast_in_dim.4), calls=%async_computation.2 | async-start | bytes 6291456 | tf_op jit(solution)/shard_map/all_to_all | solution.py:65
  98.3 7.0 %multiply_convert_fusion = (bf16[384,1024]{1,0:T(8,128)(2,1)S(1)}, f32[384,1024]{1,0:T(8,128)S(1)}) fusion(bf16[384,4096]{1,0:T(8,128)(2,1)} %collective-permute-done.10, bf16[1,4096,2048]{2,1,0:T(8,128)(2,1)} %param.6, s32[]{:T(128)S(6)} %select_n.136), kind=kOutput, calls=%fused_computation.47 | convolution fusion | flops 3223191552 | bytes 13893636 | tf_op jit(solution)/shard_map/dot_general | solution.py:69
  110.8 5.0 %collective-permute-done.14 = bf16[384,1024]{1,0:T(8,128)(2,1)} collective-permute-done((bf16[384,1024]{1,0:T(8,128)(2,1)}, bf16[384,1024]{1,0:T(8,128)(2,1)}, u32[]{:S(2)}, u32[]{:S(2)}) %collective-permute-start.14) | collective-permute-done | bytes 786464 | tf_op jit(solution)/shard_map/ppermute | solution.py:30
  116.3 10.4 %fusion.8 = bf16[384,4096]{1,0:T(8,128)(2,1)} fusion(bf16[384,1024]{1,0:T(8,128)(2,1)S(1)} %multiply_convert_fusion.1, bf16[1,4096,2048]{2,1,0:T(8,128)(2,1)} %param.6, s32[]{:T(128)S(6)} %select_n.136), kind=kOutput, calls=%fused_computation.9 | convolution fusion | flops 3222798336 | bytes 12320772 | tf_op jit(solution)/shard_map/dot_general | solution.py:69
  126.7 6.1 %collective-permute-done.12 = bf16[384,1024]{1,0:T(8,128)(2,1)S(1)} collective-permute-done((bf16[384,1024]{1,0:T(8,128)(2,1)S(1)}, bf16[384,1024]{1,0:T(8,128)(2,1)S(1)}, u32[]{:S(2)}, u32[]{:S(2)}) %collective-permute-start.12) | collective-permute-done | bytes 786464 | tf_op jit(solution)/shard_map/ppermute | solution.py:30
  133.7 14.2 %collective-permute-done.15 = bf16[384,1024]{1,0:T(8,128)(2,1)} collective-permute-done((bf16[384,1024]{1,0:T(8,128)(2,1)S(1)}, bf16[384,1024]{1,0:T(8,128)(2,1)}, u32[]{:S(2)}, u32[]{:S(2)}) %collective-permute-start.15) | collective-permute-done | bytes 786464 | tf_op jit(solution)/shard_map/ppermute | solution.py:30
  157.4 13.1 %all-to-all-start.3 = ((bf16[16,24,1024]{2,1,0:T(8,128)(2,1)}), bf16[16,24,1024]{2,1,0:T(8,128)(2,1)S(1)}, u32[]{:S(2)}, u32[]{:S(2)}) async-start(bf16[16,24,1024]{2,1,0:T(8,128)(2,1)} %bitcast.24), calls=%async_computation.3 | async-start | bytes 1572864 | tf_op jit(solution)/shard_map/all_to_all | solution.py:179
  170.5 4.1 %copy.65 = bf16[16,4,24,1024]{3,2,0,1:T(8,128)(2,1)} copy(bf16[16,4,24,1024]{3,2,1,0:T(8,128)(2,1)} %all-to-all-done.2) | data formatting | bytes 6291456 | tf_op jit(solution)/shard_map/optimization_barrier | solution.py:180
  180.1 3.3 %slice.42 = bf16[3,16,24,1024]{3,2,1,0:T(8,128)(2,1)} slice(bf16[4,16,24,1024]{3,2,1,0:T(8,128)(2,1)} %bitcast.75.clone.2), slice={[0:3], [0:16], [0:24], [0:1024]} | slice | bytes 4718592 | tf_op jit(solution)/shard_map/slice | solution.py:203
  183.4 6.1 %fusion = f32[384,4096]{1,0:T(8,128)S(1)} fusion(bf16[384,1024]{1,0:T(8,128)(2,1)} %multiply_convert_fusion.2, bf16[1,4096,2048]{2,1,0:T(8,128)(2,1)} %param.6, s32[]{:T(128)S(6)} %select_n.136), kind=kOutput, calls=%fused_computation | convolution fusion | flops 3221225472 | bytes 15466500 | tf_op jit(solution)/shard_map/dot_general | solution.py:69
  189.5 4.7 %add_convert_fusion = bf16[384,4096]{1,0:T(8,128)(2,1)} fusion(f32[384,4096]{1,0:T(8,128)S(1)} %fusion, bf16[384,4096]{1,0:T(8,128)(2,1)} %collective-permute-done.16), kind=kLoop, calls=%fused_computation.8 | loop fusion | flops 4718592 | bytes 12582912 | tf_op jit(solution)/shard_map/convert_element_type | solution.py:182
  195.1 8.0 %all-to-all-start.4 = ((bf16[16,24,4096]{2,1,0:T(8,128)(2,1)}), bf16[16,24,4096]{2,1,0:T(8,128)(2,1)S(1)}, u32[]{:S(2)}, u32[]{:S(2)}) async-start(bf16[16,24,4096]{2,1,0:T(8,128)(2,1)} %bitcast.100), calls=%async_computation.4 | async-start | bytes 6291456 | tf_op jit(solution)/shard_map/all_to_all | solution.py:65
  203.1 5.2 %fusion.17 = f32[1024,1024]{1,0:T(8,128)S(1)} fusion(bf16[1152,1024]{1,0:T(8,128)(2,1)} %bitcast.104, bf16[384,1024]{1,0:T(8,128)(2,1)} %collective-permute-done.14, bf16[384,1024]{1,0:T(8,128)(2,1)} %collective-permute-done.13, bf16[384,1024]{1,0:T(8,128)(2,1)} %multiply_convert_fusion.2), kind=kOutput, calls=%fused_computation.18 | convolution fusion | flops 2422996992 | bytes 8912896 | tf_op jit(solution)/shard_map/dot_general | solution.py:69
  212.2 4.9 %fusion.15 = f32[1024,1024]{1,0:T(8,128)S(1)} fusion(bf16[1536,1024]{1,0:T(8,128)(2,1)} %collective-permute-done.17, bf16[384,1024]{1,0:T(8,128)(2,1)S(1)} %copy-done.13, bf16[384,1024]{1,0:T(8,128)(2,1)} %collective-permute-done.11, bf16[384,1024]{1,0:T(8,128)(2,1)S(1)} %copy-done.11), kind=kOutput, calls=%fused_computation.16 | convolution fusion | flops 2422996992 | bytes 8912896 | tf_op jit(solution)/shard_map/dot_general | solution.py:69
  229.2 29.9 %all-to-all-done.4 = bf16[16,24,4096]{2,1,0:T(8,128)(2,1)S(1)} async-done(((bf16[16,24,4096]{2,1,0:T(8,128)(2,1)}), bf16[16,24,4096]{2,1,0:T(8,128)(2,1)S(1)}, u32[]{:S(2)}, u32[]{:S(2)}) %all-to-all-start.4) | async-done | bytes 3145760 | tf_op jit(solution)/shard_map/all_to_all | solution.py:65
  260.6 5.7 %all-to-all-start.5 = ((bf16[16,8,24]{2,1,0:T(8,128)(2,1)}), bf16[16,8,24]{2,1,0:T(8,128)(2,1)}, u32[]{:S(2)}, u32[]{:S(2)}) async-start(bf16[16,8,24]{2,1,0:T(8,128)(2,1)} %copy.48), calls=%async_computation.5 | async-start | bytes 65536 | tf_op jit(solution)/shard_map/all_to_all | solution.py:200
  266.3 4.5 %maximum_select_fusion = bf16[1,512,2048]{2,1,0:T(8,128)(2,1)} fusion(bf16[1,512,1024]{2,1,0:T(8,128)(2,1)} %bitcast.35, bf16[1,512,1024]{2,1,0:T(8,128)(2,1)} %get-tuple-element.61, pred[]{:T(512)S(6)} %eq.17), kind=kLoop, calls=%fused_computation.29 | loop fusion | flops 9437184 | bytes 4194305 | tf_op jit(solution)/shard_map/jit(_where)/select_n | solution.py:210
  (113 shorter events, 85.5 us)
Async XLA Ops:
  7.2 14.1 %collective-permute-start.1 = (bf16[24,4096]{1,0:T(8,128)(2,1)}, bf16[24,4096]{1,0:T(8,128)(2,1)S(1)}, u32[]{:S(2)}, u32[]{:S(2)}) collective-permute-start(bf16[24,4096]{1,0:T(8,128)(2,1)} %param.5), channel_id=1, source_target_pairs={{0,4},{1,5},{2,6},{3,7},{4,0},{5,1},{6,2},{7,3},{8,40},{9,41},{10,... | collective-permute-start | bytes 589832 | tf_op jit(solution)/shard_map/ppermute | solution.py:42
  10.8 10.5 %collective-permute-start = (bf16[24,4096]{1,0:T(8,128)(2,1)}, bf16[24,4096]{1,0:T(8,128)(2,1)S(1)}, u32[]{:S(2)}, u32[]{:S(2)}) collective-permute-start(bf16[24,4096]{1,0:T(8,128)(2,1)} %param.5), channel_id=1, source_target_pairs={{0,64},{1,65},{2,66},{3,67},{4,68},{5,69},{6,70},{7,71},{8,24},{9,... | collective-permute-start | bytes 589832 | tf_op jit(solution)/shard_map/ppermute | solution.py:42
  13.1 15.6 %all-to-all-start = ((bf16[16,8,24]{2,1,0:T(8,128)(2,1)}), bf16[16,8,24]{2,1,0:T(8,128)(2,1)}, u32[]{:S(2)}, u32[]{:S(2)}) async-start(bf16[16,8,24]{2,1,0:T(8,128)(2,1)} %copy.35), calls=%async_computation | async-start | bytes 65536 | tf_op jit(solution)/shard_map/all_to_all | solution.py:105
  22.4 33.5 %collective-permute-start.5 = (bf16[4,24,4096]{2,1,0:T(8,128)(2,1)S(1)}, bf16[4,24,4096]{2,1,0:T(8,128)(2,1)S(1)}, u32[]{:S(2)}, u32[]{:S(2)}) collective-permute-start(bf16[4,24,4096]{2,1,0:T(8,128)(2,1)S(1)} %pad_maximum_fusion.1.refs_0_), channel_id=1, source_target_pairs={{0,48},{1,49},{2,50},{3,51},{4,52},{5,53},{6,54},{7,55},{8,76},{9,... | collective-permute-start | bytes 2359304 | tf_op jit(solution)/shard_map/ppermute | solution.py:42
  26.7 29.2 %collective-permute-start.4 = (bf16[4,24,4096]{2,1,0:T(8,128)(2,1)S(1)}, bf16[4,24,4096]{2,1,0:T(8,128)(2,1)S(1)}, u32[]{:S(2)}, u32[]{:S(2)}) collective-permute-start(bf16[4,24,4096]{2,1,0:T(8,128)(2,1)S(1)} %pad_maximum_fusion.1.refs_0_), channel_id=1, source_target_pairs={{0,32},{1,33},{2,34},{3,35},{4,36},{5,37},{6,38},{7,39},{8,12},{9,... | collective-permute-start | bytes 2359304 | tf_op jit(solution)/shard_map/ppermute | solution.py:42
  26.7 29.2 %collective-permute-start.3 = (bf16[4,24,4096]{2,1,0:T(8,128)(2,1)S(1)}, bf16[4,24,4096]{2,1,0:T(8,128)(2,1)S(1)}, u32[]{:S(2)}, u32[]{:S(2)}) collective-permute-start(bf16[4,24,4096]{2,1,0:T(8,128)(2,1)S(1)} %pad_maximum_fusion.1.refs_0_), channel_id=1, source_target_pairs={{0,16},{1,17},{2,18},{3,19},{4,20},{5,21},{6,22},{7,23},{8,72},{9,... | collective-permute-start | bytes 2359304 | tf_op jit(solution)/shard_map/ppermute | solution.py:42
  32.7 25.5 %all-to-all-start.1 = ((bf16[16,24,1024]{2,1,0:T(8,128)(2,1)}), bf16[16,24,1024]{2,1,0:T(8,128)(2,1)}, u32[]{:S(2)}, u32[]{:S(2)}) async-start(bf16[16,24,1024]{2,1,0:T(8,128)(2,1)} %copy.37), calls=%async_computation.1 | async-start | bytes 1572864 | tf_op jit(solution)/shard_map/all_to_all | solution.py:120
  58.2 28.1 %collective-permute-start.10 = (bf16[384,4096]{1,0:T(8,128)(2,1)}, bf16[384,4096]{1,0:T(8,128)(2,1)}, u32[]{:S(2)}, u32[]{:S(2)}) collective-permute-start(bf16[384,4096]{1,0:T(8,128)(2,1)} %bitcast.98), channel_id=1, source_target_pairs={{0,8},{1,9},{2,10},{3,11},{4,12},{5,13},{6,14},{7,15},{8,0},{9,1},... | collective-permute-start | bytes 9437192 | tf_op jit(solution)/shard_map/ppermute | solution.py:30
  59.8 20.0 %collective-permute-start.9 = (bf16[2,4,2,24,1024]{4,3,2,1,0:T(8,128)(2,1)}, bf16[2,4,2,24,1024]{4,3,2,1,0:T(8,128)(2,1)S(1)}, u32[]{:S(2)}, u32[]{:S(2)}) collective-permute-start(bf16[2,4,2,24,1024]{4,3,2,1,0:T(8,128)(2,1)} %bitcast.12), channel_id=1, source_target_pairs={{0,4},{1,5},{2,6},{3,7},{4,0},{5,1},{6,2},{7,3},{8,12},{9,13},{10,... | collective-permute-start | bytes 2359304 | tf_op jit(solution)/shard_map/ppermute | solution.py:30
  88.4 59.4 %all-to-all-start.2 = ((bf16[16,4,24,1024]{3,2,1,0:T(8,128)(2,1)}), bf16[16,4,24,1024]{3,2,1,0:T(8,128)(2,1)}, u32[]{:S(2)}, u32[]{:S(2)}) async-start(bf16[16,4,24,1024]{3,2,1,0:T(8,128)(2,1)} %broadcast_in_dim.4), calls=%async_computation.2 | async-start | bytes 6291456 | tf_op jit(solution)/shard_map/all_to_all | solution.py:65
  96.1 19.8 %collective-permute-start.14 = (bf16[384,1024]{1,0:T(8,128)(2,1)}, bf16[384,1024]{1,0:T(8,128)(2,1)}, u32[]{:S(2)}, u32[]{:S(2)}) collective-permute-start(bf16[384,1024]{1,0:T(8,128)(2,1)} %multiply_convert_fusion.2), channel_id=1, source_target_pairs={{0,3},{1,2},{2,1},{3,0},{4,7},{5,6},{6,5},{7,4},{8,11},{9,10},{10,... | collective-permute-start | bytes 2359304 | tf_op jit(solution)/shard_map/ppermute | solution.py:30
  98.3 18.0 %collective-permute-start.13 = (bf16[384,1024]{1,0:T(8,128)(2,1)}, bf16[384,1024]{1,0:T(8,128)(2,1)}, u32[]{:S(2)}, u32[]{:S(2)}) collective-permute-start(bf16[384,1024]{1,0:T(8,128)(2,1)} %multiply_convert_fusion.2), channel_id=1, source_target_pairs={{0,1},{1,0},{2,3},{3,2},{4,5},{5,4},{6,7},{7,6},{8,9},{9,8},{10,11... | collective-permute-start | bytes 2359304 | tf_op jit(solution)/shard_map/ppermute | solution.py:30
  106.6 26.1 %collective-permute-start.12 = (bf16[384,1024]{1,0:T(8,128)(2,1)S(1)}, bf16[384,1024]{1,0:T(8,128)(2,1)S(1)}, u32[]{:S(2)}, u32[]{:S(2)}) collective-permute-start(bf16[384,1024]{1,0:T(8,128)(2,1)S(1)} %multiply_convert_fusion.1), channel_id=1, source_target_pairs={{0,3},{1,2},{2,1},{3,0},{4,7},{5,6},{6,5},{7,4},{8,11},{9,10},{10,... | collective-permute-start | bytes 2359304 | tf_op jit(solution)/shard_map/ppermute | solution.py:30
  107.7 25.5 %collective-permute-start.11 = (bf16[384,1024]{1,0:T(8,128)(2,1)S(1)}, bf16[384,1024]{1,0:T(8,128)(2,1)}, u32[]{:S(2)}, u32[]{:S(2)}) collective-permute-start(bf16[384,1024]{1,0:T(8,128)(2,1)S(1)} %multiply_convert_fusion.1), channel_id=1, source_target_pairs={{0,1},{1,0},{2,3},{3,2},{4,5},{5,4},{6,7},{7,6},{8,9},{9,8},{10,11... | collective-permute-start | bytes 2359304 | tf_op jit(solution)/shard_map/ppermute | solution.py:30
  109.5 38.3 %collective-permute-start.15 = (bf16[384,1024]{1,0:T(8,128)(2,1)S(1)}, bf16[384,1024]{1,0:T(8,128)(2,1)}, u32[]{:S(2)}, u32[]{:S(2)}) collective-permute-start(bf16[384,1024]{1,0:T(8,128)(2,1)S(1)} %bitcast.111), channel_id=1, source_target_pairs={{0,4},{1,5},{2,6},{3,7},{4,0},{5,1},{6,2},{7,3},{8,12},{9,13},{10,... | collective-permute-start | bytes 2359304 | tf_op jit(solution)/shard_map/ppermute | solution.py:30
  147.9 41.6 %collective-permute-start.16 = (bf16[384,4096]{1,0:T(8,128)(2,1)}, bf16[384,4096]{1,0:T(8,128)(2,1)}, u32[]{:S(2)}, u32[]{:S(2)}) collective-permute-start(bf16[384,4096]{1,0:T(8,128)(2,1)} %fusion.8), channel_id=1, source_target_pairs={{0,8},{1,9},{2,10},{3,11},{4,12},{5,13},{6,14},{7,15},{8,0},{9,1},... | collective-permute-start | bytes 9437192 | tf_op jit(solution)/shard_map/ppermute | solution.py:30
  153.9 55.6 %collective-permute-start.18 = (bf16[384,1024]{1,0:T(8,128)(2,1)}, bf16[384,1024]{1,0:T(8,128)(2,1)}, u32[]{:S(2)}, u32[]{:S(2)}) collective-permute-start(bf16[384,1024]{1,0:T(8,128)(2,1)} %collective-permute-done.14), channel_id=1, source_target_pairs={{0,1},{1,0},{2,3},{3,2},{4,5},{5,4},{6,7},{7,6},{8,9},{9,8},{10,11... | collective-permute-start | bytes 2359304 | tf_op jit(solution)/shard_map/ppermute | solution.py:30
  157.4 36.8 %all-to-all-start.3 = ((bf16[16,24,1024]{2,1,0:T(8,128)(2,1)}), bf16[16,24,1024]{2,1,0:T(8,128)(2,1)S(1)}, u32[]{:S(2)}, u32[]{:S(2)}) async-start(bf16[16,24,1024]{2,1,0:T(8,128)(2,1)} %bitcast.24), calls=%async_computation.3 | async-start | bytes 1572864 | tf_op jit(solution)/shard_map/all_to_all | solution.py:179
  170.4 104.8 %reduce-scatter.2.cloned.1.call-start = ((), (), s32[]{:S(2)}) async-start(), calls=%async_computation.7 | async-start | bytes 2621440 | tf_op jit(solution)/shard_map/reduce_scatter | solution.py:189
  174.6 37.5 %collective-permute-start.17 = (bf16[1536,1024]{1,0:T(8,128)(2,1)}, bf16[1536,1024]{1,0:T(8,128)(2,1)}, u32[]{:S(2)}, u32[]{:S(2)}) collective-permute-start(bf16[1536,1024]{1,0:T(8,128)(2,1)} %bitcast.31), channel_id=1, source_target_pairs={{0,8},{1,9},{2,10},{3,11},{4,12},{5,13},{6,14},{7,15},{8,0},{9,1},... | collective-permute-start | bytes 9437192 | tf_op jit(solution)/shard_map/ppermute | solution.py:30
  177.9 39.1 %collective-permute-start.19 = (bf16[384,1024]{1,0:T(8,128)(2,1)}, bf16[384,1024]{1,0:T(8,128)(2,1)}, u32[]{:S(2)}, u32[]{:S(2)}) collective-permute-start(bf16[384,1024]{1,0:T(8,128)(2,1)} %collective-permute-done.11), channel_id=1, source_target_pairs={{0,3},{1,2},{2,1},{3,0},{4,7},{5,6},{6,5},{7,4},{8,11},{9,10},{10,... | collective-permute-start | bytes 2359304 | tf_op jit(solution)/shard_map/ppermute | solution.py:30
  195.1 64.0 %all-to-all-start.4 = ((bf16[16,24,4096]{2,1,0:T(8,128)(2,1)}), bf16[16,24,4096]{2,1,0:T(8,128)(2,1)S(1)}, u32[]{:S(2)}, u32[]{:S(2)}) async-start(bf16[16,24,4096]{2,1,0:T(8,128)(2,1)} %bitcast.100), calls=%async_computation.4 | async-start | bytes 6291456 | tf_op jit(solution)/shard_map/all_to_all | solution.py:65
  221.6 44.7 %collective-permute-start.20 = (bf16[512,1024]{1,0:T(8,128)(2,1)}, bf16[512,1024]{1,0:T(8,128)(2,1)}, u32[]{:S(2)}, u32[]{:S(2)}) collective-permute-start(bf16[512,1024]{1,0:T(8,128)(2,1)} %get-tuple-element.62), channel_id=1, source_target_pairs={{0,4},{1,5},{2,6},{3,7},{4,0},{5,1},{6,2},{7,3},{8,12},{9,13},{10,... | collective-permute-start | bytes 3145736 | tf_op jit(solution)/shard_map/ppermute | solution.py:30
  260.6 13.1 %all-to-all-start.5 = ((bf16[16,8,24]{2,1,0:T(8,128)(2,1)}), bf16[16,8,24]{2,1,0:T(8,128)(2,1)}, u32[]{:S(2)}, u32[]{:S(2)}) async-start(bf16[16,8,24]{2,1,0:T(8,128)(2,1)} %copy.48), calls=%async_computation.5 | async-start | bytes 65536 | tf_op jit(solution)/shard_map/all_to_all | solution.py:200
  (18 other events, 91.0 us)
Sparse Core Ops, SparseCore 0:
  178.0 39.0 reduce-scatter.1
